TPU v7x, 512 devices: a whole 4x8x8 slice. The times are simulated.
512 devices in a mesh: node: 64 (over y, x, core), board: 8 (over z).
Axes of the slice: x: 4, y: 8, z: 8, core: 2. Of those that a mesh axis runs over, the one named last changes fastest.
Arguments:
- logits: float32 [8, 4, 2048, 1326], P('board', None, 'node'), may hold values from -310 to 310
- pot_size: float32 [4, 2048], P(None, 'node'), may hold values from 1 to 20
- node_type: int32 [4, 2048], P(None, 'node'), may hold values from 0 to 2, as said below
- parent_slot: int32 [4, 2048], P(None, 'node'), may hold values from 0 to 2047, as said below
- range_one: float32 [8, 1326], P('board'), may hold values from 0.05 to 1
- range_two: float32 [8, 1326], P('board'), may hold values from 0.05 to 1
- hand_rank: int32 [8, 1326], P('board'), may hold values from 0 to 7461
- live_mask: int32 [8, 1326], P('board'), may hold values 0 or 1
Outputs:
- new_logits: float32 [8, 4, 2048, 1326], P('board', None, 'node')
- values_half: float32 [8, 4, 2048, 1326], P('board', None, 'node')
Inputs may be any that keep to these rules, and one draw needn't show every extreme that they name: `node_type`: 0 marks an inner node. At each level but the last, each aligned group of four slots holds exactly one node of type 0; the last level holds none. `parent_slot`: at level 0 every entry is 0. At a level above 0 the four nodes of an aligned group of four share one parent, a node of type 0 at the level before, and every such node is the parent of exactly one group; the parent's group index is the group's own index minus an offset of 0 to 7, one offset a level, modulo 2048 / 4.
All inputs are finite; a program needn't handle non-finite values. No bound on the sum of `live_mask` on one device may be relied on, other than what follows from the above.
Results may differ from a plain program's by a relative error of at most 0.0003.
Values sent between devices are 32-bit elements; how exact they have to be, the bound alone decides.
A program may use at most 64 MiB of HBM per device.

v0:
```python
import functools

import jax
import jax.numpy as jnp
import numpy as np
from jax import lax
from jax.sharding import Mesh
from jax.sharding import PartitionSpec as P

HANDS = 1326
LEVELS = 4
SLOT_DEV = 32
NODE = ("node_0", "node_1", "node_2")
NODE_BOARD = ("node_0", "node_1", "node_2", "board")


step_scale = 0.5
eps_value = 1e-06


def passed_along(value, axis, steps):
    count = lax.axis_size(axis)
    pairs = [(source, (source + steps) % count) for source in range(count)]
    return lax.ppermute(value, axis, pairs)


def one_axis_at_a_time(value, axes):
    return functools.reduce(lax.psum, axes, value)


def card_pairs(hand_count):
    low_list = []
    high_list = []
    for low_card in range(52):
        for high_card in range(low_card + 1, 52):
            low_list.append(low_card)
            high_list.append(high_card)
    return (np.array(low_list[:hand_count], np.int32), np.array(high_list[:hand_count], np.int32))


def payoff_blocks(hand_rank, live_mask):
    low_np, high_np = card_pairs(hand_rank.shape[-1])
    low_card = jnp.asarray(low_np)
    high_card = jnp.asarray(high_np)
    clash_mask = (
        (low_card[:, None] == low_card[None, :])
        | (low_card[:, None] == high_card[None, :])
        | (high_card[:, None] == low_card[None, :])
        | (high_card[:, None] == high_card[None, :])
    )
    alive_flag = live_mask > 0
    keep_pair = jnp.logical_not(clash_mask)[None] & alive_flag[:, :, None] & alive_flag[:, None, :]
    higher = hand_rank[:, :, None] > hand_rank[:, None, :]
    lower = hand_rank[:, :, None] < hand_rank[:, None, :]
    order_value = jnp.where(higher, 1.0, jnp.where(lower, -1.0, 0.0))
    show_block = jnp.where(keep_pair, order_value, 0.0).astype(jnp.bfloat16)
    compat_block = jnp.where(keep_pair, 1.0, 0.0).astype(jnp.bfloat16)
    return (show_block, compat_block)


def policy(logits):
    full_shape = logits.shape
    grouped = logits.reshape(full_shape[0], full_shape[1], full_shape[2] // 4, 4, full_shape[3])
    return jax.nn.softmax(grouped, axis=3).reshape(full_shape)


def inner_position(kind_row):
    groups = SLOT_DEV // 4
    kind_grid = kind_row.reshape(groups, 4)
    return jnp.sum(jnp.where(kind_grid == 0, jnp.arange(4, dtype=jnp.int32)[None, :], 0), axis=1)


def reach_levels(strategy, parent_slot, node_type, range_one, range_two, start_slot):
    slot_count = SLOT_DEV * lax.axis_size(NODE)
    groups = SLOT_DEV // 4
    reach_one = range_one[:, None, :] * strategy[:, 0]
    reach_two = jnp.broadcast_to(range_two[:, None, :], reach_one.shape)
    list_one = [reach_one]
    list_two = [reach_two]
    for depth_idx in range(1, LEVELS):
        rel_slot = (parent_slot[depth_idx] - start_slot + SLOT_DEV) % slot_count
        inner_pos = inner_position(node_type[depth_idx - 1])
        tail_pos = 4 * jnp.arange(1, groups, dtype=jnp.int32) + inner_pos[1:]
        tail_one = jnp.take(reach_one, tail_pos, axis=1)
        tail_two = jnp.take(reach_two, tail_pos, axis=1)
        before_one, before_two = passed_along((tail_one, tail_two), NODE, 1)
        local_idx = jnp.where(
            rel_slot >= SLOT_DEV, rel_slot - SLOT_DEV + groups - 1, rel_slot // 4 - 1
        )
        window_one = jnp.concatenate([before_one, reach_one], axis=1)
        window_two = jnp.concatenate([before_two, reach_two], axis=1)
        above_one = jnp.take(window_one, local_idx, axis=1)
        above_two = jnp.take(window_two, local_idx, axis=1)
        if depth_idx % 2 == 0:
            reach_one = above_one * strategy[:, depth_idx]
            reach_two = above_two
        else:
            reach_one = above_one
            reach_two = above_two * strategy[:, depth_idx]
        list_one.append(reach_one)
        list_two.append(reach_two)
    return (jnp.stack(list_one, axis=1), jnp.stack(list_two, axis=1))


def terminal_pay(reach_one, reach_two, pot_size, node_type, show_block, compat_block):
    boards = reach_one.shape[0]
    column_count = LEVELS * SLOT_DEV
    level_sign = jnp.where(jnp.arange(LEVELS) % 2 == 0, -1.0, 1.0).astype(jnp.float32)
    show_scale = jnp.where(node_type == 2, pot_size, 0.0)
    fold_scale = jnp.where(node_type == 1, pot_size, 0.0) * level_sign[:, None]

    def columns(reach_value, scale_value):
        return (
            (reach_value * scale_value[None, :, :, None])
            .astype(jnp.bfloat16)
            .reshape(boards, column_count, HANDS)
        )

    show_cols = jnp.concatenate(
        [columns(reach_two, show_scale), columns(reach_one, show_scale)], axis=1
    )
    fold_cols = jnp.concatenate(
        [columns(reach_two, fold_scale), -columns(reach_one, fold_scale)], axis=1
    )
    product = jnp.einsum(
        "bij,bnj->bni", show_block, show_cols, preferred_element_type=jnp.float32
    ) + jnp.einsum("bij,bnj->bni", compat_block, fold_cols, preferred_element_type=jnp.float32)
    pay_one = product[:, :column_count].reshape(boards, LEVELS, SLOT_DEV, HANDS)
    pay_two = product[:, column_count:].reshape(boards, LEVELS, SLOT_DEV, HANDS)
    return (pay_one, pay_two)


def values_up(strategy, parent_slot, node_type, pay_one, pay_two, start_slot):
    boards = strategy.shape[0]
    slot_count = SLOT_DEV * lax.axis_size(NODE)
    groups = SLOT_DEV // 4
    value_one = pay_one[:, LEVELS - 1]
    value_two = pay_two[:, LEVELS - 1]
    found_list = [None] * LEVELS
    found_list[LEVELS - 1] = value_two
    for depth_idx in range(LEVELS - 2, -1, -1):
        child_level = depth_idx + 1
        weight = strategy[:, child_level]
        if child_level % 2 == 0:
            term_one = weight * value_one
            term_two = value_two
        else:
            term_one = value_one
            term_two = weight * value_two
        group_one = term_one.reshape(boards, groups, 4, HANDS).sum(axis=2)
        group_two = term_two.reshape(boards, groups, 4, HANDS).sum(axis=2)
        parent_group = parent_slot[child_level].reshape(groups, 4)[:, 0]
        local_idx = (parent_group - start_slot + SLOT_DEV) % slot_count
        keeper = (jnp.arange(SLOT_DEV, 2 * SLOT_DEV)[:, None] == local_idx[None, :]).astype(
            jnp.float32
        )
        own_one = jnp.einsum("jg,bgh->bjh", keeper, group_one, precision=lax.Precision.HIGHEST)
        own_two = jnp.einsum("jg,bgh->bjh", keeper, group_two, precision=lax.Precision.HIGHEST)
        far_placer = (
            (local_idx[None, :] < SLOT_DEV)
            & (local_idx[None, :] // 4 - 1 == jnp.arange(groups - 1)[:, None])
        ).astype(jnp.float32)
        far_one = jnp.einsum("kg,bgh->bkh", far_placer, group_one, precision=lax.Precision.HIGHEST)
        far_two = jnp.einsum("kg,bgh->bkh", far_placer, group_two, precision=lax.Precision.HIGHEST)
        got_one, got_two = passed_along((far_one, far_two), NODE, -1)
        kind_here = node_type[depth_idx]
        landing = (
            (jnp.arange(SLOT_DEV)[:, None] // 4 == jnp.arange(1, groups)[None, :])
            & (kind_here[:, None] == 0)
        ).astype(jnp.float32)
        sent_one = jnp.einsum("sk,bkh->bsh", landing, got_one, precision=lax.Precision.HIGHEST)
        sent_two = jnp.einsum("sk,bkh->bsh", landing, got_two, precision=lax.Precision.HIGHEST)
        value_one = pay_one[:, depth_idx] + (own_one + sent_one)
        value_two = pay_two[:, depth_idx] + (own_two + sent_two)
        found_list[depth_idx] = value_one if depth_idx % 2 == 0 else value_two
    return jnp.stack(found_list, axis=1)


def operate(
    point,
    pot_size,
    node_type,
    parent_slot,
    range_one,
    range_two,
    show_block,
    compat_block,
    start_slot,
):
    strategy = policy(point)
    reach_one, reach_two = reach_levels(
        strategy, parent_slot, node_type, range_one, range_two, start_slot
    )
    pay_one, pay_two = terminal_pay(
        reach_one, reach_two, pot_size, node_type, show_block, compat_block
    )
    return values_up(strategy, parent_slot, node_type, pay_one, pay_two, start_slot)


def rate_for(values_found):
    square_sum = one_axis_at_a_time(jnp.sum(values_found * values_found), NODE_BOARD)
    entry_count = values_found.size * lax.axis_size(NODE) * lax.axis_size("board")
    return step_scale / jnp.sqrt(square_sum / entry_count + eps_value)


def per_device(
    logits, pot_size, node_type, parent_slot, range_one, range_two, hand_rank, live_mask
):
    show_block, compat_block = payoff_blocks(hand_rank, live_mask)
    start_slot = lax.axis_index(NODE) * SLOT_DEV
    current = logits
    anchor_mix = 1.0 / 2
    base_point = current + anchor_mix * (logits - current)
    values_now = operate(
        current,
        pot_size,
        node_type,
        parent_slot,
        range_one,
        range_two,
        show_block,
        compat_block,
        start_slot,
    )
    half_point = base_point + rate_for(values_now) * values_now
    values_half = operate(
        half_point,
        pot_size,
        node_type,
        parent_slot,
        range_one,
        range_two,
        show_block,
        compat_block,
        start_slot,
    )
    current = base_point + rate_for(values_half) * values_half
    return (current, values_half)


def solution(mesh):
    finer = Mesh(
        mesh.devices.reshape(8, 4, 2, mesh.shape["board"]), ("node_0", "node_1", "node_2", "board")
    )
    placed = (
        P("board", None, NODE, None),
        P(None, NODE),
        P(None, NODE),
        P(None, NODE),
        P("board", None),
        P("board", None),
        P("board", None),
        P("board", None),
    )
    return jax.shard_map(
        per_device,
        mesh=finer,
        in_specs=placed,
        out_specs=(P("board", None, NODE, None), P("board", None, NODE, None)),
        check_vma=False,
    )
```

profile of v0, /device:TPU:1, one launch (start us, length us, event | category | flops | bytes accessed | tf_op | source)
XLA Modules:
  0.0 289.9 jit_solution(5622177818438568045)
XLA Ops:
  3.7 4.5 %collective-permute-start = (f32[1,7,1326]{2,1,0:T(8,128)S(1)}, f32[1,7,1326]{2,1,0:T(8,128)S(1)}, u32[]{:S(2)}, u32[]{:S(2)}) collective-permute-start(f32[1,7,1326]{2,1,0:T(8,128)S(1)} %bitcast_select_fusion.21), channel_id=1, source_target_pairs={{0,8},{8,16},{16,24},{24,32},{32,40},{40,48},{48,56},{56,64},{64,7... | collective-permute-start | bytes 111392 | tf_op jit(solution)/shard_map/ppermute | solution.py:24
  17.5 1.9 collective-permute-start.1
  19.7 4.7 %collective-permute-done.1 = f32[1,7,1326]{2,1,0:T(8,128)S(1)} collective-permute-done((f32[1,7,1326]{2,1,0:T(8,128)S(1)}, f32[1,7,1326]{2,1,0:T(8,128)S(1)}, u32[]{:S(2)}, u32[]{:S(2)}) %collective-permute-start.1) | collective-permute-done | bytes 37160 | tf_op jit(solution)/shard_map/ppermute | solution.py:24
  25.8 1.9 collective-permute-start.2
  27.8 6.7 %collective-permute-done.2 = f32[1,7,1326]{2,1,0:T(8,128)S(1)} collective-permute-done((f32[1,7,1326]{2,1,0:T(8,128)S(1)}, f32[1,7,1326]{2,1,0:T(8,128)S(1)}, u32[]{:S(2)}, u32[]{:S(2)}) %collective-permute-start.2) | collective-permute-done | bytes 37160 | tf_op jit(solution)/shard_map/ppermute | solution.py:24
  35.9 1.9 collective-permute-start.3
  37.9 6.7 %collective-permute-done.3 = f32[1,7,1326]{2,1,0:T(8,128)S(1)} collective-permute-done((f32[1,7,1326]{2,1,0:T(8,128)S(1)}, f32[1,7,1326]{2,1,0:T(8,128)S(1)}, u32[]{:S(2)}, u32[]{:S(2)}) %collective-permute-start.3) | collective-permute-done | bytes 37160 | tf_op jit(solution)/shard_map/ppermute | solution.py:24
  46.0 1.9 collective-permute-start.4
  48.0 6.7 %collective-permute-done.4 = f32[1,7,1326]{2,1,0:T(8,128)S(1)} collective-permute-done((f32[1,7,1326]{2,1,0:T(8,128)S(1)}, f32[1,7,1326]{2,1,0:T(8,128)S(1)}, u32[]{:S(2)}, u32[]{:S(2)}) %collective-permute-start.4) | collective-permute-done | bytes 37160 | tf_op jit(solution)/shard_map/ppermute | solution.py:24
  56.1 2.1 collective-permute-start.5
  58.3 6.5 %collective-permute-done.5 = f32[1,7,1326]{2,1,0:T(8,128)S(1)} collective-permute-done((f32[1,7,1326]{2,1,0:T(8,128)S(1)}, f32[1,7,1326]{2,1,0:T(8,128)S(1)}, u32[]{:S(2)}, u32[]{:S(2)}) %collective-permute-start.5) | collective-permute-done | bytes 37160 | tf_op jit(solution)/shard_map/ppermute | solution.py:24
  67.1 3.7 %fusion.35 = f32[256,1326]{0,1:T(8,128)S(1)} fusion(s32[1326]{0:T(1024)S(1)} %reduce.22, pred[1326]{0:T(1024)(128)(4,1)S(1)} %compare_reduce_fusion, s32[1326]{0:T(1024)S(1)} %copy-done.61, s32[1326]{0:T(1024)S(1)} %copy-done.63, bf16[1,128,1326]{2,1,0:T(8,128)(2,1)S(1)} %get-tuple-element.58, bf16[1,128,1326]{2,1,0:T(8,128)(2,1)S(1)} %get-tuple-element.43), kind=kOutput, calls=%fused_computation.82 | convolution fusion | flops 929727552 | bytes 2053974 | tf_op jit(solution)/shard_map/bij,bnj->bni/dot_general | solution.py:125
  70.7 3.5 %fusion.9 = f32[1,256,1326]{1,2,0:T(8,128)S(1)} fusion(f32[256,1326]{0,1:T(8,128)S(1)} %fusion.35, s32[1326]{0:T(1024)S(1)} %copy-done.61, s32[1326]{0:T(1024)S(1)} %copy-done.63, pred[1326]{0:T(1024)(128)(4,1)S(1)} %compare_reduce_fusion, bf16[1,128,1326]{2,1,0:T(8,128)(2,1)S(1)} %fusion.56, bf16[1,128,1326]{2,1,0:T(8,128)(2,1)S(1)} %get-tuple-element.42), kind=kOutput, calls=%fused_computation.34 | convolution fusion | flops 923033920 | bytes 3406494 | tf_op jit(solution)/shard_map/bij,bnj->bni/dot_general | solution.py:127
  77.6 8.0 %collective-permute-start.6 = (f32[1,7,1326]{2,1,0:T(8,128)}, f32[1,7,1326]{2,1,0:T(8,128)S(1)}, u32[]{:S(2)}, u32[]{:S(2)}) collective-permute-start(f32[1,7,1326]{2,1,0:T(8,128)} %convolution_bitcast_fusion.9), channel_id=1, source_target_pairs={{0,504},{8,0},{16,8},{24,16},{32,24},{40,32},{48,40},{56,48},{64,5... | collective-permute-start | bytes 111392 | tf_op jit(solution)/shard_map/ppermute | solution.py:24
  87.6 1.7 slice_multiply_fusion.3
  90.5 1.6 fusion.90
  92.1 1.4 convolution_bitcast_fusion.6
  93.5 1.9 collective-permute-start.9
  99.2 1.9 collective-permute-start.7
  103.0 1.9 collective-permute-start.10
  105.9 3.1 %collective-permute-start.8 = (f32[1,7,1326]{2,1,0:T(8,128)S(1)}, f32[1,7,1326]{2,1,0:T(8,128)S(1)}, u32[]{:S(2)}, u32[]{:S(2)}) collective-permute-start(f32[1,7,1326]{2,1,0:T(8,128)S(1)} %convolution_bitcast_fusion.7), channel_id=1, source_target_pairs={{0,504},{8,0},{16,8},{24,16},{32,24},{40,32},{48,40},{56,48},{64,5... | collective-permute-start | bytes 111392 | tf_op jit(solution)/shard_map/ppermute | solution.py:24
  109.3 1.9 collective-permute-done.8
  112.3 11.3 %psum.56 = f32[]{:T(128)} all-reduce(f32[]{:T(128)} %multiply_reduce_fusion.1), channel_id=1, replica_groups=mesh['node_0'=8,'node_1'=4,'node_2'=2,'board'=8] {'node_0'}, use_global_device_ids=true, to_apply=%region_11.14 | all-reduce | flops 1 | bytes 8 | tf_op jit(solution)/shard_map/psum | solution.py:28
  123.6 12.8 %psum.57 = f32[]{:T(128)} all-reduce(f32[]{:T(128)} %psum.56), channel_id=1, replica_groups=mesh['node_0'=8,'node_1'=4,'node_2'=2,'board'=8] {'node_1'}, use_global_device_ids=true, to_apply=%region_12.15 | all-reduce | flops 1 | bytes 8 | tf_op jit(solution)/shard_map/psum | solution.py:28
  136.4 3.1 %psum.58 = f32[]{:T(128)} all-reduce(f32[]{:T(128)} %psum.57), channel_id=1, replica_groups=mesh['node_0'=8,'node_1'=4,'node_2'=2,'board'=8] {'node_2'}, use_global_device_ids=true, to_apply=%region_13.16 | all-reduce | flops 1 | bytes 8 | tf_op jit(solution)/shard_map/psum | solution.py:28
  139.5 16.0 %psum.59 = f32[]{:T(128)} all-reduce(f32[]{:T(128)} %psum.58), channel_id=1, replica_groups=mesh['node_0'=8,'node_1'=4,'node_2'=2,'board'=8] {'board'}, use_global_device_ids=true, to_apply=%region_14.17 | all-reduce | flops 1 | bytes 8 | tf_op jit(solution)/shard_map/psum | solution.py:28
  160.7 7.5 %collective-permute-start.11 = (f32[1,7,1326]{2,1,0:T(8,128)S(1)}, f32[1,7,1326]{2,1,0:T(8,128)S(1)}, u32[]{:S(2)}, u32[]{:S(2)}) collective-permute-start(f32[1,7,1326]{2,1,0:T(8,128)S(1)} %bitcast_select_fusion.15), channel_id=1, source_target_pairs={{0,8},{8,16},{16,24},{24,32},{32,40},{40,48},{48,56},{56,64},{64,7... | collective-permute-start | bytes 111392 | tf_op jit(solution)/shard_map/ppermute | solution.py:24
  171.1 4.2 %collective-permute-start.12 = (f32[1,7,1326]{2,1,0:T(8,128)S(1)}, f32[1,7,1326]{2,1,0:T(8,128)S(1)}, u32[]{:S(2)}, u32[]{:S(2)}) collective-permute-start(f32[1,7,1326]{2,1,0:T(8,128)S(1)} %bitcast_select_fusion.14), channel_id=1, source_target_pairs={{0,8},{8,16},{16,24},{24,32},{32,40},{40,48},{48,56},{56,64},{64,7... | collective-permute-start | bytes 111392 | tf_op jit(solution)/shard_map/ppermute | solution.py:24
  175.4 2.3 collective-permute-done.12
  179.5 2.9 %collective-permute-start.13 = (f32[1,7,1326]{2,1,0:T(8,128)S(1)}, f32[1,7,1326]{2,1,0:T(8,128)S(1)}, u32[]{:S(2)}, u32[]{:S(2)}) collective-permute-start(f32[1,7,1326]{2,1,0:T(8,128)S(1)} %bitcast_select_fusion.13), channel_id=1, source_target_pairs={{0,8},{8,16},{16,24},{24,32},{32,40},{40,48},{48,56},{56,64},{64,7... | collective-permute-start | bytes 111392 | tf_op jit(solution)/shard_map/ppermute | solution.py:24
  182.5 5.7 %collective-permute-done.13 = f32[1,7,1326]{2,1,0:T(8,128)S(1)} collective-permute-done((f32[1,7,1326]{2,1,0:T(8,128)S(1)}, f32[1,7,1326]{2,1,0:T(8,128)S(1)}, u32[]{:S(2)}, u32[]{:S(2)}) %collective-permute-start.13) | collective-permute-done | bytes 37160 | tf_op jit(solution)/shard_map/ppermute | solution.py:24
  189.8 1.9 collective-permute-start.14
  191.8 6.7 %collective-permute-done.14 = f32[1,7,1326]{2,1,0:T(8,128)S(1)} collective-permute-done((f32[1,7,1326]{2,1,0:T(8,128)S(1)}, f32[1,7,1326]{2,1,0:T(8,128)S(1)}, u32[]{:S(2)}, u32[]{:S(2)}) %collective-permute-start.14) | collective-permute-done | bytes 37160 | tf_op jit(solution)/shard_map/ppermute | solution.py:24
  200.2 1.9 collective-permute-start.15
  202.2 6.7 %collective-permute-done.15 = f32[1,7,1326]{2,1,0:T(8,128)S(1)} collective-permute-done((f32[1,7,1326]{2,1,0:T(8,128)S(1)}, f32[1,7,1326]{2,1,0:T(8,128)S(1)}, u32[]{:S(2)}, u32[]{:S(2)}) %collective-permute-start.15) | collective-permute-done | bytes 37160 | tf_op jit(solution)/shard_map/ppermute | solution.py:24
  211.0 3.6 %fusion.34 = f32[256,1326]{0,1:T(8,128)S(1)} fusion(s32[1326]{0:T(1024)S(1)} %copy-done.37, pred[1326]{0:T(1024)(128)(4,1)S(1)} %copy-done.60, s32[1326]{0:T(1024)S(1)} %copy-done.62, s32[1326]{0:T(1024)S(1)} %copy-done.64, bf16[1,128,1326]{2,1,0:T(8,128)(2,1)S(1)} %get-tuple-element.59, bf16[1,128,1326]{2,1,0:T(8,128)(2,1)S(1)} %get-tuple-element.37), kind=kOutput, calls=%fused_computation.81 | convolution fusion | flops 929727552 | bytes 2053974 | tf_op jit(solution)/shard_map/bij,bnj->bni/dot_general | solution.py:125
  214.7 3.5 %fusion.8 = f32[1,256,1326]{1,2,0:T(8,128)S(1)} fusion(f32[256,1326]{0,1:T(8,128)S(1)} %fusion.34, s32[1326]{0:T(1024)S(1)} %copy-done.62, s32[1326]{0:T(1024)S(1)} %copy-done.64, pred[1326]{0:T(1024)(128)(4,1)S(1)} %copy-done.60, bf16[1,128,1326]{2,1,0:T(8,128)(2,1)S(1)} %fusion.57, bf16[1,128,1326]{2,1,0:T(8,128)(2,1)S(1)} %get-tuple-element.36), kind=kOutput, calls=%fused_computation.33 | convolution fusion | flops 923033920 | bytes 3406494 | tf_op jit(solution)/shard_map/bij,bnj->bni/dot_general | solution.py:127
  220.0 8.0 %collective-permute-start.16 = (f32[1,7,1326]{2,1,0:T(8,128)}, f32[1,7,1326]{2,1,0:T(8,128)S(1)}, u32[]{:S(2)}, u32[]{:S(2)}) collective-permute-start(f32[1,7,1326]{2,1,0:T(8,128)} %convolution_bitcast_fusion.4), channel_id=1, source_target_pairs={{0,504},{8,0},{16,8},{24,16},{32,24},{40,32},{48,40},{56,48},{64,5... | collective-permute-start | bytes 111392 | tf_op jit(solution)/shard_map/ppermute | solution.py:24
  229.2 1.6 slice_multiply_fusion.1
  231.4 1.9 collective-permute-start.19
  235.0 1.9 collective-permute-start.17
  238.6 3.6 %collective-permute-start.20 = (f32[1,7,1326]{2,1,0:T(8,128)S(1)}, f32[1,7,1326]{2,1,0:T(8,128)S(1)}, u32[]{:S(2)}, u32[]{:S(2)}) collective-permute-start(f32[1,7,1326]{2,1,0:T(8,128)S(1)} %convolution_bitcast_fusion), channel_id=1, source_target_pairs={{0,504},{8,0},{16,8},{24,16},{32,24},{40,32},{48,40},{56,48},{64,5... | collective-permute-start | bytes 111392 | tf_op jit(solution)/shard_map/ppermute | solution.py:24
  243.1 3.6 %collective-permute-start.18 = (f32[1,7,1326]{2,1,0:T(8,128)S(1)}, f32[1,7,1326]{2,1,0:T(8,128)S(1)}, u32[]{:S(2)}, u32[]{:S(2)}) collective-permute-start(f32[1,7,1326]{2,1,0:T(8,128)S(1)} %convolution_bitcast_fusion.2), channel_id=1, source_target_pairs={{0,504},{8,0},{16,8},{24,16},{32,24},{40,32},{48,40},{56,48},{64,5... | collective-permute-start | bytes 111392 | tf_op jit(solution)/shard_map/ppermute | solution.py:24
  247.0 1.5 collective-permute-done.18
  249.6 11.3 %psum.60 = f32[]{:T(128)} all-reduce(f32[]{:T(128)} %get-tuple-element.10), channel_id=1, replica_groups=mesh['node_0'=8,'node_1'=4,'node_2'=2,'board'=8] {'node_0'}, use_global_device_ids=true, to_apply=%region_23.26 | all-reduce | flops 1 | bytes 8 | tf_op jit(solution)/shard_map/psum | solution.py:28
  260.9 12.9 %psum.61 = f32[]{:T(128)} all-reduce(f32[]{:T(128)} %psum.60), channel_id=1, replica_groups=mesh['node_0'=8,'node_1'=4,'node_2'=2,'board'=8] {'node_1'}, use_global_device_ids=true, to_apply=%region_24.27 | all-reduce | flops 1 | bytes 8 | tf_op jit(solution)/shard_map/psum | solution.py:28
  273.8 3.1 %psum.62 = f32[]{:T(128)} all-reduce(f32[]{:T(128)} %psum.61), channel_id=1, replica_groups=mesh['node_0'=8,'node_1'=4,'node_2'=2,'board'=8] {'node_2'}, use_global_device_ids=true, to_apply=%region_25.28 | all-reduce | flops 1 | bytes 8 | tf_op jit(solution)/shard_map/psum | solution.py:28
  276.9 11.3 %psum.63 = f32[]{:T(128)} all-reduce(f32[]{:T(128)} %psum.62), channel_id=1, replica_groups=mesh['node_0'=8,'node_1'=4,'node_2'=2,'board'=8] {'board'}, use_global_device_ids=true, to_apply=%region_26.29 | all-reduce | flops 1 | bytes 8 | tf_op jit(solution)/shard_map/psum | solution.py:28
  (334 shorter events, 59.1 us)
Async XLA Ops:
  0.6 9.0 %copy-start = (f32[1,4,32,1326]{3,2,1,0:T(8,128)S(1)}, f32[1,4,32,1326]{3,2,1,0:T(8,128)}, u32[]{:S(2)}) copy-start(f32[1,4,32,1326]{3,2,1,0:T(8,128)} %param.14) | copy-start | bytes 2036740
  2.3 33.5 %copy-start.44 = (pred[7]{0:T(512)(128)(4,1)}, pred[7]{0:T(512)(128)(4,1)S(1)}, u32[]{:S(2)}) copy-start(pred[7]{0:T(512)(128)(4,1)S(1)} %get-tuple-element.28) | copy-start | bytes 25
  2.3 32.9 %copy-start.38 = (s32[1024]{0:T(1024)}, s32[1024]{0:T(1024)S(1)}, u32[]{:S(2)}) copy-start(s32[1024]{0:T(1024)S(1)} %pad_clamp_fusion.5) | copy-start | bytes 12292
  3.7 12.3 %collective-permute-start = (f32[1,7,1326]{2,1,0:T(8,128)S(1)}, f32[1,7,1326]{2,1,0:T(8,128)S(1)}, u32[]{:S(2)}, u32[]{:S(2)}) collective-permute-start(f32[1,7,1326]{2,1,0:T(8,128)S(1)} %bitcast_select_fusion.21), channel_id=1, source_target_pairs={{0,8},{8,16},{16,24},{24,32},{32,40},{40,48},{48,56},{56,64},{64,7... | collective-permute-start | bytes 111392 | tf_op jit(solution)/shard_map/ppermute | solution.py:24
  9.9 60.8 %copy-start.59 = (pred[1326]{0:T(1024)(128)(4,1)}, pred[1326]{0:T(1024)(128)(4,1)S(1)}, u32[]{:S(2)}) copy-start(pred[1326]{0:T(1024)(128)(4,1)S(1)} %compare_reduce_fusion) | copy-start | bytes 3982
  10.2 35.7 %copy-start.34 = (pred[7]{0:T(512)(128)(4,1)}, pred[7]{0:T(512)(128)(4,1)S(1)}, u32[]{:S(2)}) copy-start(pred[7]{0:T(512)(128)(4,1)S(1)} %get-tuple-element.24) | copy-start | bytes 25
  10.5 45.5 %copy-start.32 = (pred[7]{0:T(512)(128)(4,1)}, pred[7]{0:T(512)(128)(4,1)S(1)}, u32[]{:S(2)}) copy-start(pred[7]{0:T(512)(128)(4,1)S(1)} %get-tuple-element.20) | copy-start | bytes 25
  10.6 54.2 %copy-start.14 = (s32[1024]{0:T(1024)}, s32[1024]{0:T(1024)S(1)}, u32[]{:S(2)}) copy-start(s32[1024]{0:T(1024)S(1)} %pad_clamp_fusion) | copy-start | bytes 12292
  10.6 44.9 %copy-start.15 = (s32[1024]{0:T(1024)}, s32[1024]{0:T(1024)S(1)}, u32[]{:S(2)}) copy-start(s32[1024]{0:T(1024)S(1)} %pad_clamp_fusion.1) | copy-start | bytes 12292
  10.6 34.7 %copy-start.17 = (s32[1024]{0:T(1024)}, s32[1024]{0:T(1024)S(1)}, u32[]{:S(2)}) copy-start(s32[1024]{0:T(1024)S(1)} %pad_clamp_fusion.3) | copy-start | bytes 12292
  10.7 44.0 %copy-start.16 = (s32[1024]{0:T(1024)}, s32[1024]{0:T(1024)S(1)}, u32[]{:S(2)}) copy-start(s32[1024]{0:T(1024)S(1)} %pad_clamp_fusion.2) | copy-start | bytes 12292
  10.7 33.9 %copy-start.39 = (s32[1024]{0:T(1024)}, s32[1024]{0:T(1024)S(1)}, u32[]{:S(2)}) copy-start(s32[1024]{0:T(1024)S(1)} %pad_clamp_fusion.4) | copy-start | bytes 12292
  13.5 63.3 %copy-start.25 = (pred[8]{0:T(512)(128)(4,1)}, pred[8]{0:T(512)(128)(4,1)S(1)}, u32[]{:S(2)}) copy-start(pred[8]{0:T(512)(128)(4,1)S(1)} %get-tuple-element.16) | copy-start | bytes 28
  13.5 72.0 %copy-start.27 = (s32[8]{0:T(128)}, s32[8]{0:T(128)S(1)}, u32[]{:S(2)}) copy-start(s32[8]{0:T(128)S(1)} %get-tuple-element.17) | copy-start | bytes 100
  13.5 63.3 %copy-start.29 = (s32[8]{0:T(128)}, s32[8]{0:T(128)S(1)}, u32[]{:S(2)}) copy-start(s32[8]{0:T(128)S(1)} %fusion.189) | copy-start | bytes 100
  17.5 6.9 %collective-permute-start.1 = (f32[1,7,1326]{2,1,0:T(8,128)S(1)}, f32[1,7,1326]{2,1,0:T(8,128)S(1)}, u32[]{:S(2)}, u32[]{:S(2)}) collective-permute-start(f32[1,7,1326]{2,1,0:T(8,128)S(1)} %bitcast_select_fusion.20), channel_id=1, source_target_pairs={{0,8},{8,16},{16,24},{24,32},{32,40},{40,48},{48,56},{56,64},{64,7... | collective-permute-start | bytes 111392 | tf_op jit(solution)/shard_map/ppermute | solution.py:24
  19.6 46.8 %copy-start.46 = (f32[128]{0:T(128)}, f32[128]{0:T(128)S(1)}, u32[]{:S(2)}) copy-start(f32[128]{0:T(128)S(1)} %mul.327) | copy-start | bytes 1540
  19.6 46.9 %copy-start.36 = (s32[1326]{0:T(1024)}, s32[1326]{0:T(1024)S(1)}, u32[]{:S(2)}) copy-start(s32[1326]{0:T(1024)S(1)} %reduce.22) | copy-start | bytes 15916
  25.8 8.7 %collective-permute-start.2 = (f32[1,7,1326]{2,1,0:T(8,128)S(1)}, f32[1,7,1326]{2,1,0:T(8,128)S(1)}, u32[]{:S(2)}, u32[]{:S(2)}) collective-permute-start(f32[1,7,1326]{2,1,0:T(8,128)S(1)} %bitcast_select_fusion.19), channel_id=1, source_target_pairs={{0,8},{8,16},{16,24},{24,32},{32,40},{40,48},{48,56},{56,64},{64,7... | collective-permute-start | bytes 111392 | tf_op jit(solution)/shard_map/ppermute | solution.py:24
  35.9 8.7 %collective-permute-start.3 = (f32[1,7,1326]{2,1,0:T(8,128)S(1)}, f32[1,7,1326]{2,1,0:T(8,128)S(1)}, u32[]{:S(2)}, u32[]{:S(2)}) collective-permute-start(f32[1,7,1326]{2,1,0:T(8,128)S(1)} %bitcast_select_fusion.18), channel_id=1, source_target_pairs={{0,8},{8,16},{16,24},{24,32},{32,40},{40,48},{48,56},{56,64},{64,7... | collective-permute-start | bytes 111392 | tf_op jit(solution)/shard_map/ppermute | solution.py:24
  46.0 8.7 %collective-permute-start.4 = (f32[1,7,1326]{2,1,0:T(8,128)S(1)}, f32[1,7,1326]{2,1,0:T(8,128)S(1)}, u32[]{:S(2)}, u32[]{:S(2)}) collective-permute-start(f32[1,7,1326]{2,1,0:T(8,128)S(1)} %bitcast_select_fusion.17), channel_id=1, source_target_pairs={{0,8},{8,16},{16,24},{24,32},{32,40},{40,48},{48,56},{56,64},{64,7... | collective-permute-start | bytes 111392 | tf_op jit(solution)/shard_map/ppermute | solution.py:24
  56.1 8.7 %collective-permute-start.5 = (f32[1,7,1326]{2,1,0:T(8,128)S(1)}, f32[1,7,1326]{2,1,0:T(8,128)S(1)}, u32[]{:S(2)}, u32[]{:S(2)}) collective-permute-start(f32[1,7,1326]{2,1,0:T(8,128)S(1)} %bitcast_select_fusion.16), channel_id=1, source_target_pairs={{0,8},{8,16},{16,24},{24,32},{32,40},{40,48},{48,56},{56,64},{64,7... | collective-permute-start | bytes 111392 | tf_op jit(solution)/shard_map/ppermute | solution.py:24
  77.6 17.8 %collective-permute-start.6 = (f32[1,7,1326]{2,1,0:T(8,128)}, f32[1,7,1326]{2,1,0:T(8,128)S(1)}, u32[]{:S(2)}, u32[]{:S(2)}) collective-permute-start(f32[1,7,1326]{2,1,0:T(8,128)} %convolution_bitcast_fusion.9), channel_id=1, source_target_pairs={{0,504},{8,0},{16,8},{24,16},{32,24},{40,32},{48,40},{56,48},{64,5... | collective-permute-start | bytes 111392 | tf_op jit(solution)/shard_map/ppermute | solution.py:24
  89.3 11.9 %copy-start.4 = (f32[1,128,1326]{2,1,0:T(8,128)S(1)}, f32[1,128,1326]{2,1,0:T(8,128)}, u32[]{:S(2)}) copy-start(f32[1,128,1326]{2,1,0:T(8,128)} %copy.21) | copy-start | bytes 2036740
  93.5 7.7 %collective-permute-start.9 = (f32[1,7,1326]{2,1,0:T(8,128)}, f32[1,7,1326]{2,1,0:T(8,128)S(1)}, u32[]{:S(2)}, u32[]{:S(2)}) collective-permute-start(f32[1,7,1326]{2,1,0:T(8,128)} %convolution_bitcast_fusion.6), channel_id=1, source_target_pairs={{0,504},{8,0},{16,8},{24,16},{32,24},{40,32},{48,40},{56,48},{64,5... | collective-permute-start | bytes 111392 | tf_op jit(solution)/shard_map/ppermute | solution.py:24
  96.4 8.6 %copy-start.12 = (pred[32]{0:T(512)(128)(4,1)S(1)}, pred[32]{0:T(512)(128)(4,1)}, u32[]{:S(2)}) copy-start(pred[32]{0:T(512)(128)(4,1)} %get-tuple-element.53) | copy-start | bytes 100
  99.2 5.7 %collective-permute-start.7 = (f32[1,7,1326]{2,1,0:T(8,128)S(1)}, f32[1,7,1326]{2,1,0:T(8,128)S(1)}, u32[]{:S(2)}, u32[]{:S(2)}) collective-permute-start(f32[1,7,1326]{2,1,0:T(8,128)S(1)} %convolution_bitcast_fusion.8), channel_id=1, source_target_pairs={{0,504},{8,0},{16,8},{24,16},{32,24},{40,32},{48,40},{56,48},{64,5... | collective-permute-start | bytes 111392 | tf_op jit(solution)/shard_map/ppermute | solution.py:24
  102.4 8.8 %copy-start.49 = (pred[32]{0:T(512)(128)(4,1)S(1)}, pred[32]{0:T(512)(128)(4,1)}, u32[]{:S(2)}) copy-start(pred[32]{0:T(512)(128)(4,1)} %get-tuple-element.48) | copy-start | bytes 100
  103.0 6.0 %collective-permute-start.10 = (f32[1,7,1326]{2,1,0:T(8,128)S(1)}, f32[1,7,1326]{2,1,0:T(8,128)S(1)}, u32[]{:S(2)}, u32[]{:S(2)}) collective-permute-start(f32[1,7,1326]{2,1,0:T(8,128)S(1)} %convolution_bitcast_fusion.5), channel_id=1, source_target_pairs={{0,504},{8,0},{16,8},{24,16},{32,24},{40,32},{48,40},{56,48},{64,5... | collective-permute-start | bytes 111392 | tf_op jit(solution)/shard_map/ppermute | solution.py:24
  105.9 5.4 %collective-permute-start.8 = (f32[1,7,1326]{2,1,0:T(8,128)S(1)}, f32[1,7,1326]{2,1,0:T(8,128)S(1)}, u32[]{:S(2)}, u32[]{:S(2)}) collective-permute-start(f32[1,7,1326]{2,1,0:T(8,128)S(1)} %convolution_bitcast_fusion.7), channel_id=1, source_target_pairs={{0,504},{8,0},{16,8},{24,16},{32,24},{40,32},{48,40},{56,48},{64,5... | collective-permute-start | bytes 111392 | tf_op jit(solution)/shard_map/ppermute | solution.py:24
  111.5 44.6 %copy-start.2 = (f32[1,1,32,1326]{3,2,1,0:T(8,128)}, f32[1,1,32,1326]{3,2,1,0:T(8,128)S(1)}, u32[]{:S(2)}) copy-start(f32[1,1,32,1326]{3,2,1,0:T(8,128)S(1)} %fusion.31) | copy-start | bytes 509188
  160.7 8.7 %collective-permute-start.11 = (f32[1,7,1326]{2,1,0:T(8,128)S(1)}, f32[1,7,1326]{2,1,0:T(8,128)S(1)}, u32[]{:S(2)}, u32[]{:S(2)}) collective-permute-start(f32[1,7,1326]{2,1,0:T(8,128)S(1)} %bitcast_select_fusion.15), channel_id=1, source_target_pairs={{0,8},{8,16},{16,24},{24,32},{32,40},{40,48},{48,56},{56,64},{64,7... | collective-permute-start | bytes 111392 | tf_op jit(solution)/shard_map/ppermute | solution.py:24
  171.1 6.6 %collective-permute-start.12 = (f32[1,7,1326]{2,1,0:T(8,128)S(1)}, f32[1,7,1326]{2,1,0:T(8,128)S(1)}, u32[]{:S(2)}, u32[]{:S(2)}) collective-permute-start(f32[1,7,1326]{2,1,0:T(8,128)S(1)} %bitcast_select_fusion.14), channel_id=1, source_target_pairs={{0,8},{8,16},{16,24},{24,32},{32,40},{40,48},{48,56},{56,64},{64,7... | collective-permute-start | bytes 111392 | tf_op jit(solution)/shard_map/ppermute | solution.py:24
  179.5 8.7 %collective-permute-start.13 = (f32[1,7,1326]{2,1,0:T(8,128)S(1)}, f32[1,7,1326]{2,1,0:T(8,128)S(1)}, u32[]{:S(2)}, u32[]{:S(2)}) collective-permute-start(f32[1,7,1326]{2,1,0:T(8,128)S(1)} %bitcast_select_fusion.13), channel_id=1, source_target_pairs={{0,8},{8,16},{16,24},{24,32},{32,40},{40,48},{48,56},{56,64},{64,7... | collective-permute-start | bytes 111392 | tf_op jit(solution)/shard_map/ppermute | solution.py:24
  189.8 8.7 %collective-permute-start.14 = (f32[1,7,1326]{2,1,0:T(8,128)S(1)}, f32[1,7,1326]{2,1,0:T(8,128)S(1)}, u32[]{:S(2)}, u32[]{:S(2)}) collective-permute-start(f32[1,7,1326]{2,1,0:T(8,128)S(1)} %bitcast_select_fusion.12), channel_id=1, source_target_pairs={{0,8},{8,16},{16,24},{24,32},{32,40},{40,48},{48,56},{56,64},{64,7... | collective-permute-start | bytes 111392 | tf_op jit(solution)/shard_map/ppermute | solution.py:24
  200.2 8.7 %collective-permute-start.15 = (f32[1,7,1326]{2,1,0:T(8,128)S(1)}, f32[1,7,1326]{2,1,0:T(8,128)S(1)}, u32[]{:S(2)}, u32[]{:S(2)}) collective-permute-start(f32[1,7,1326]{2,1,0:T(8,128)S(1)} %bitcast_select_fusion.11), channel_id=1, source_target_pairs={{0,8},{8,16},{16,24},{24,32},{32,40},{40,48},{48,56},{56,64},{64,7... | collective-permute-start | bytes 111392 | tf_op jit(solution)/shard_map/ppermute | solution.py:24
  220.0 13.3 %collective-permute-start.16 = (f32[1,7,1326]{2,1,0:T(8,128)}, f32[1,7,1326]{2,1,0:T(8,128)S(1)}, u32[]{:S(2)}, u32[]{:S(2)}) collective-permute-start(f32[1,7,1326]{2,1,0:T(8,128)} %convolution_bitcast_fusion.4), channel_id=1, source_target_pairs={{0,504},{8,0},{16,8},{24,16},{32,24},{40,32},{48,40},{56,48},{64,5... | collective-permute-start | bytes 111392 | tf_op jit(solution)/shard_map/ppermute | solution.py:24
  231.4 5.5 %collective-permute-start.19 = (f32[1,7,1326]{2,1,0:T(8,128)S(1)}, f32[1,7,1326]{2,1,0:T(8,128)}, u32[]{:S(2)}, u32[]{:S(2)}) collective-permute-start(f32[1,7,1326]{2,1,0:T(8,128)S(1)} %convolution_bitcast_fusion.1), channel_id=1, source_target_pairs={{0,504},{8,0},{16,8},{24,16},{32,24},{40,32},{48,40},{56,48},{64,5... | collective-permute-start | bytes 111392 | tf_op jit(solution)/shard_map/ppermute | solution.py:24
  234.3 7.9 %copy-start.13 = (pred[32]{0:T(512)(128)(4,1)S(1)}, pred[32]{0:T(512)(128)(4,1)}, u32[]{:S(2)}) copy-start(pred[32]{0:T(512)(128)(4,1)} %get-tuple-element.53) | copy-start | bytes 100
  234.9 8.0 %copy-start.52 = (pred[8]{0:T(512)(128)(4,1)S(1)}, pred[8]{0:T(512)(128)(4,1)}, u32[]{:S(2)}) copy-start(pred[8]{0:T(512)(128)(4,1)} %get-tuple-element.12) | copy-start | bytes 28
  234.9 8.0 %copy-start.54 = (s32[8]{0:T(128)S(1)}, s32[8]{0:T(128)}, u32[]{:S(2)}) copy-start(s32[8]{0:T(128)} %fusion.187) | copy-start | bytes 100
  235.0 7.2 %collective-permute-start.17 = (f32[1,7,1326]{2,1,0:T(8,128)S(1)}, f32[1,7,1326]{2,1,0:T(8,128)S(1)}, u32[]{:S(2)}, u32[]{:S(2)}) collective-permute-start(f32[1,7,1326]{2,1,0:T(8,128)S(1)} %convolution_bitcast_fusion.3), channel_id=1, source_target_pairs={{0,504},{8,0},{16,8},{24,16},{32,24},{40,32},{48,40},{56,48},{64,5... | collective-permute-start | bytes 111392 | tf_op jit(solution)/shard_map/ppermute | solution.py:24
  238.0 10.5 %copy-start.50 = (pred[32]{0:T(512)(128)(4,1)S(1)}, pred[32]{0:T(512)(128)(4,1)}, u32[]{:S(2)}) copy-start(pred[32]{0:T(512)(128)(4,1)} %get-tuple-element.48) | copy-start | bytes 100
  238.4 10.3 %copy-start.10 = (f32[1,1,32,1326]{3,2,1,0:T(8,128)S(1)}, f32[1,1,32,1326]{3,2,1,0:T(8,128)}, u32[]{:S(2)}) copy-start(f32[1,1,32,1326]{3,2,1,0:T(8,128)} %get-tuple-element.35) | copy-start | bytes 509188
  238.5 10.3 %copy-start.11 = (f32[1,32,1326]{2,1,0:T(8,128)S(1)}, f32[1,32,1326]{2,1,0:T(8,128)}, u32[]{:S(2)}) copy-start(f32[1,32,1326]{2,1,0:T(8,128)} %get-tuple-element.63) | copy-start | bytes 509188
  238.6 8.1 %collective-permute-start.20 = (f32[1,7,1326]{2,1,0:T(8,128)S(1)}, f32[1,7,1326]{2,1,0:T(8,128)S(1)}, u32[]{:S(2)}, u32[]{:S(2)}) collective-permute-start(f32[1,7,1326]{2,1,0:T(8,128)S(1)} %convolution_bitcast_fusion), channel_id=1, source_target_pairs={{0,504},{8,0},{16,8},{24,16},{32,24},{40,32},{48,40},{56,48},{64,5... | collective-permute-start | bytes 111392 | tf_op jit(solution)/shard_map/ppermute | solution.py:24
  243.1 5.4 %collective-permute-start.18 = (f32[1,7,1326]{2,1,0:T(8,128)S(1)}, f32[1,7,1326]{2,1,0:T(8,128)S(1)}, u32[]{:S(2)}, u32[]{:S(2)}) collective-permute-start(f32[1,7,1326]{2,1,0:T(8,128)S(1)} %convolution_bitcast_fusion.2), channel_id=1, source_target_pairs={{0,504},{8,0},{16,8},{24,16},{32,24},{40,32},{48,40},{56,48},{64,5... | collective-permute-start | bytes 111392 | tf_op jit(solution)/shard_map/ppermute | solution.py:24
  249.6 40.3 %copy-start.1 = (f32[1,4,32,1326]{3,2,1,0:T(8,128)}, f32[1,4,32,1326]{3,2,1,0:T(8,128)S(1)}, u32[]{:S(2)}) copy-start(f32[1,4,32,1326]{3,2,1,0:T(8,128)S(1)} %get-tuple-element.11) | copy-start | bytes 2036740
  (38 other events, 112.9 us)
where the time goes:
time: 295 us; the launch traced here: 290 us
  blocking collectives  81.7 us (28%)
  starting transfers between devices  68.5 us (23%)
  waiting for transfers between devices  57.1 us (19%)
  matrix products  30.2 us (10%)
  local copies, waits for them, and re-layouts  28.8 us (10%)
  other arithmetic  19.7 us (7%)
  between operations  3.9 us (1%)
    psum x8, blocking collectives, one_axis_at_a_time(): return functools.reduce(lax.psum, axes, value)  81.7 us
    ppermute x21, starting transfers between devices, passed_along(): return lax.ppermute(value, axis, pairs)  68.5 us
    ppermute x21, waiting for transfers between devices, passed_along(): return lax.ppermute(value, axis, pairs)  57.1 us
    dot_general x2, matrix products, terminal_pay(): jnp.einsum('bij,bnj->bni', show_block, show_cols, preferred_element_type=...  7.3 us
    dot_general x2, matrix products, terminal_pay(): jnp.einsum('bij,bnj->bni', compat_block, fold_cols, preferred_element_typ...  7.08 us
  transfers between devices with their start and end apart: 21, of which 12 were waited for; matrix products, arithmetic and copies ran while one was open for 10% of the time, Pallas kernels for 0%

commit v1 on v0

v1 whole, which is shorter than its diff:
```python
import functools

import jax
import jax.numpy as jnp
import numpy as np
from jax import lax
from jax.experimental import pallas as pl
from jax.experimental.pallas import tpu as pltpu
from jax.sharding import PartitionSpec as P

HANDS = 1326
PAD = 1408
CHUNKS = PAD // 128
LEVELS = 4
SLOT_DEV = 32
GROUPS = SLOT_DEV // 4
NODES = 64
BOARDS = 8
ALL_GROUPS = NODES * GROUPS
ENTRIES = BOARDS * LEVELS * NODES * SLOT_DEV * HANDS
STEP_SCALE = 0.5
EPS = 1e-06
ROWS = 48 * 3
ROWS_ALL = ROWS + 32
F32 = jnp.float32
BF16 = jnp.bfloat16
MESH = pl.DeviceIdType.MESH


def card_rows():
    table = np.zeros((64, PAD), np.float32)
    hand = 0
    for low in range(52):
        for high in range(low + 1, 52):
            if hand < HANDS:
                table[low, hand] = 1.0
                table[high, hand] = 1.0
                hand += 1
    return table


def iota(shape, dim):
    return lax.broadcasted_iota(jnp.int32, shape, dim)


def pick_rows(onehot, rows):
    high = rows.astype(BF16)
    rest = rows - high.astype(F32)
    mid = rest.astype(BF16)
    low = (rest - mid.astype(F32)).astype(BF16)
    parts = jnp.concatenate([high, mid, low], axis=0)
    pick = jnp.where(onehot, 1.0, 0.0)
    pick = jnp.concatenate([pick, pick, pick], axis=1).astype(BF16)
    return jnp.dot(pick, parts, preferred_element_type=F32)


def kernel(
    logits,
    pot,
    kind,
    parent,
    range_one,
    range_two,
    rank,
    live,
    cards,
    out_logits,
    out_values,
    own,
    own_pot,
    own_kind,
    parent_s,
    rng1,
    rng2,
    rank_v,
    live_v,
    cards_v,
    win0,
    win2,
    win3a,
    win3b,
    pot0,
    pot2,
    pot3,
    kind0,
    kind2,
    kind3,
    reach1,
    reach2,
    rank_p,
    dead_p,
    lhs_cards,
    rhs_cards,
    table,
    zbuf,
    strat,
    qbuf,
    cols,
    blocks,
    pay,
    part_a,
    part_b,
    ring_a1,
    ring_b1,
    ring_a2,
    ring_b2,
    ret0,
    ret2,
    ret3a,
    ret3b,
    fin_values,
    fin_logits,
    in_sem,
    out_sem,
    halo_send,
    halo_recv,
    ret_send,
    ret_recv,
    ar_send_a,
    ar_send_b,
    ar_recv_a1,
    ar_recv_b1,
    ar_recv_a2,
    ar_recv_b2,
):
    node = lax.axis_index("node")
    board = lax.axis_index("board")
    core = lax.rem(node, 2)
    chip = node // 2

    def at_node(step):
        return {"node": lax.rem(node + step + NODES, NODES), "board": board}

    def peer_a(j):
        spot = lax.rem(board * 2 + core + j, 16)
        return {"node": chip * 2 + lax.rem(spot, 2), "board": spot // 2}

    def peer_b(j):
        return {"node": lax.rem(chip + j, 32) * 2 + core, "board": board}

    barrier = pltpu.get_barrier_semaphore()
    for step in (1, -1, 2, -2):
        pl.semaphore_signal(barrier, inc=1, device_id=at_node(step), device_id_type=MESH)

    @pl.loop(1, 16)
    def _(j):
        pl.semaphore_signal(barrier, inc=1, device_id=peer_a(j), device_id_type=MESH)

    @pl.loop(1, 32)
    def _(j):
        pl.semaphore_signal(barrier, inc=1, device_id=peer_b(j), device_id_type=MESH)

    loads = [
        pltpu.make_async_copy(src, dst, in_sem.at[idx])
        for idx, (src, dst) in enumerate(
            [
                (live, live_v),
                (rank, rank_v),
                (cards, cards_v),
                (pot, own_pot),
                (kind, own_kind),
                (parent, parent_s),
                (range_one, rng1),
                (range_two, rng2),
                (logits.at[0], own),
            ]
        )
    ]
    for load in loads:
        load.start()
    for load in loads:
        load.wait()

    def halo(idx, src, dst, step):
        return pltpu.make_async_remote_copy(
            src_ref=src,
            dst_ref=dst,
            send_sem=halo_send.at[idx],
            recv_sem=halo_recv.at[idx],
            device_id=at_node(step),
            device_id_type=MESH,
        )

    halos = [
        halo(0, pot, pot0, 1),
        halo(1, kind, kind0, 1),
        halo(2, pot, pot2, -1),
        halo(3, kind, kind2, -1),
        halo(4, pot, pot3, -2),
        halo(5, kind, kind3, -2),
        halo(6, logits.at[0, 0], win0, 1),
        halo(7, logits.at[0, 2], win2, -1),
        halo(8, logits.at[0, 3], win3a, -1),
        halo(9, logits.at[0, 3, pl.ds(0, 24)], win3b, -2),
    ]
    pl.semaphore_wait(barrier, 4 + 15 + 31)
    for copy in halos:
        copy.start()

    zero_row = jnp.zeros((1, PAD), F32)
    reach1[...] = zero_row
    reach2[...] = zero_row
    rank_p[...] = zero_row
    alive = jnp.where(live_v[...] > 0, 1.0, 0.0)
    reach1[:, 0:HANDS] = rng1[...] * alive
    reach2[:, 0:HANDS] = rng2[...] * alive
    rank_p[:, 0:HANDS] = rank_v[...].astype(F32)
    dead_p[...] = jnp.ones((1, PAD), F32)
    dead_p[:, 0:HANDS] = 1.0 - alive
    dead = dead_p[...]
    lhs_cards[0:48] = cards_v[0:48].astype(BF16)
    rhs_cards[0:48] = cards_v[0:48].astype(BF16)
    tail = cards_v[48:64]
    row = iota((16, PAD), 0)
    lhs_cards[48:64] = jnp.where(row == 4, 1.0, jnp.where(row == 5, dead, tail)).astype(BF16)
    rhs_cards[48:64] = jnp.where(row == 4, dead, jnp.where(row == 5, 1.0, tail)).astype(BF16)

    @pl.loop(0, CHUNKS)
    def _(jb):
        base = pl.multiple_of(jb * 128, 128)
        shared = lax.dot_general(
            lhs_cards[:, pl.ds(base, 128)],
            rhs_cards[...],
            (((0,), (0,)), ((), ())),
            preferred_element_type=F32,
        )
        rank_j = jnp.broadcast_to(rank_p[:, pl.ds(base, 128)], (128, 128)).T
        for ic in range(CHUNKS):
            span = slice(ic * 128, ic * 128 + 128)
            keep = shared[:, span] < 0.5
            order = jnp.clip(rank_p[:, span] - rank_j, -1.0, 1.0)
            blocks[pl.ds(base, 128), span] = jnp.where(keep, order, 0.0).astype(BF16)
            blocks[pl.ds(PAD + base, 128), span] = jnp.where(keep, 1.0, 0.0).astype(BF16)

    def offset(level):
        return jnp.bitwise_and(node * GROUPS - parent_s[level, 0] // 4 + ALL_GROUPS, ALL_GROUPS - 1)

    off1 = offset(1)
    off2 = offset(2)
    off23 = off2 + offset(3)

    for copy in halos[:6]:
        copy.wait()

    lane = iota((8, SLOT_DEV), 1)
    group = iota((8, SLOT_DEV), 0)

    def fill_table(level, shift, windows):
        for k in range(4):
            target = 4 * (group + shift) + k
            pots = jnp.zeros((8, SLOT_DEV), F32)
            kinds = jnp.zeros((8, SLOT_DEV), F32)
            for base, pot_ref, kind_ref in windows:
                hit = lane + base == target
                pots += jnp.where(hit, pot_ref[level : level + 1], 0.0)
                kinds += jnp.where(hit, kind_ref[level : level + 1].astype(F32), 0.0)
            pots = jnp.broadcast_to(jnp.sum(pots, axis=1, keepdims=True), (8, 128))
            kinds = jnp.broadcast_to(jnp.sum(kinds, axis=1, keepdims=True), (8, 128))
            sign = -1.0 if level % 2 == 0 else 1.0
            table[0, level, k] = jnp.where(kinds > 1.5, pots, 0.0)
            table[1, level, k] = jnp.where(jnp.abs(kinds - 1.0) < 0.5, pots, 0.0) * sign
            table[2, level, k] = jnp.where(kinds < 0.5, 1.0, 0.0)

    fill_table(0, -off1, [(-SLOT_DEV, pot0, kind0), (0, own_pot, own_kind)])
    fill_table(1, 0, [(0, own_pot, own_kind)])
    fill_table(2, off2, [(0, own_pot, own_kind), (SLOT_DEV, pot2, kind2)])
    fill_table(
        3,
        off23,
        [(0, own_pot, own_kind), (SLOT_DEV, pot2, kind2), (2 * SLOT_DEV, pot3, kind3)],
    )

    def gather(level, shift, rows):
        count = rows.shape[0]
        out_row = iota((32, count), 0)
        col = iota((32, count), 1)
        want = 4 * (jnp.bitwise_and(out_row, 7) + shift) + out_row // 8
        zbuf[level, :, PAD - 128 : PAD] = jnp.zeros((32, 128), F32)
        zbuf[level, :, 0:HANDS] = pick_rows(col == want, rows)

    gather(1, 0, own[1])
    halos[6].wait()
    gather(0, 8 - off1, jnp.concatenate([win0[...], own[0]], axis=0))
    halos[7].wait()
    gather(2, off2, jnp.concatenate([own[2], win2[...]], axis=0))
    halos[8].wait()
    halos[9].wait()
    gather(
        3,
        off23,
        jnp.concatenate([own[3], win3a[...], win3b[...], jnp.zeros((8, HANDS), F32)], axis=0),
    )

    def put(first_row, span, fold, even, odd):
        pair = jnp.concatenate([even, odd], axis=0).astype(BF16)
        cols[first_row : first_row + 16, pl.ds(span + (PAD if fold else 0), 128)] = pair

    def rounded(value):
        return value.astype(BF16).astype(F32)

    def put_sum(first_row, span, fold, value):
        high = rounded(value)
        put(first_row, span, fold, high, value - high)

    def columns(rate):
        @pl.loop(0, CHUNKS)
        def _(chunk):
            span = pl.multiple_of(chunk * 128, 128)

            def soft(level):
                z = [zbuf[level, 8 * k : 8 * k + 8, pl.ds(span, 128)] for k in range(4)]
                if rate is not None:
                    z = [
                        z[k] + rate * qbuf[level, 8 * k : 8 * k + 8, pl.ds(span, 128)]
                        for k in range(4)
                    ]
                top = jnp.maximum(jnp.maximum(z[0], z[1]), jnp.maximum(z[2], z[3]))
                e = [jnp.exp(x - top) for x in z]
                inv = 1.0 / ((e[0] + e[1]) + (e[2] + e[3]))
                return [x * inv for x in e]

            def inner(level, values):
                return sum(table[2, level, k] * values[k] for k in range(4))

            def both(level, values, sign):
                show = [values[k] * table[0, level, k] for k in range(4)]
                fold = [values[k] * table[1, level, k] for k in range(4)]
                return show, [-x for x in fold] if sign < 0 else fold

            def put_slots(first_row, pairs):
                for fold, values in enumerate(pairs):
                    put(first_row, span, fold, values[0], values[1])
                    put(first_row + 16, span, fold, values[2], values[3])

            def put_sums(first_row, pairs):
                for fold, values in enumerate(pairs):
                    put_sum(first_row, span, fold, sum(rounded(x) for x in values))

            one = reach1[:, pl.ds(span, 128)]
            two = reach2[:, pl.ds(span, 128)]
            if rate is None:
                put_slots(ROWS, both(0, [two] * 4, 1))
            x1 = one * inner(0, soft(0))
            y1 = [two * s for s in soft(1)]
            y2 = inner(1, y1)
            put_slots(0, both(1, [x1] * 4, -1))
            put_sums(32, both(1, y1, 1))
            s2 = soft(2)
            x2 = [x1 * s for s in s2]
            x3 = inner(2, x2)
            put_slots(48, both(2, [y2] * 4, 1))
            put_sums(80, both(2, x2, -1))
            s3 = soft(3)
            y3 = [y2 * s for s in s3]
            put_slots(96, both(3, [x3] * 4, -1))
            put_sums(128, both(3, y3, 1))
            for k in range(4):
                strat[0, 8 * k : 8 * k + 8, pl.ds(span, 128)] = s2[k]
                strat[1, 8 * k : 8 * k + 8, pl.ds(span, 128)] = s3[k]

    def payoffs(rows):
        for first in range(0, PAD, 256):
            last = min(first + 256, PAD)
            pay[0:rows, first:last] = jnp.dot(
                cols[0:rows, :], blocks[:, first:last], preferred_element_type=F32
            )

    def values_up():
        def step(chunk, total):
            span = pl.multiple_of(chunk * 128, 128)

            def get(first_row):
                return pay[first_row : first_row + 8, pl.ds(span, 128)]

            def slots(first_row):
                return [get(first_row + 8 * k) for k in range(4)]

            def summed(first_row):
                return get(first_row) + get(first_row + 8)

            def weighted(which, values):
                return sum(
                    strat[which, 8 * k : 8 * k + 8, pl.ds(span, 128)] * values[k]
                    for k in range(4)
                )

            def joined(level, values, below):
                return [values[k] + table[2, level, k] * below for k in range(4)]

            q3 = slots(96)
            q2 = joined(2, slots(48), summed(128))
            q1 = joined(1, slots(0), summed(80) + weighted(1, q3))
            q0 = joined(0, slots(ROWS), summed(32) + weighted(0, q2))
            for level, q in enumerate((q0, q1, q2, q3)):
                for k in range(4):
                    qbuf[level, 8 * k : 8 * k + 8, pl.ds(span, 128)] = q[k]
                total = total + ((q[0] * q[0] + q[1] * q[1]) + (q[2] * q[2] + q[3] * q[3]))
            return total

        total = lax.fori_loop(0, CHUNKS, step, jnp.zeros((8, 128), F32))
        return jnp.sum(total, axis=0, keepdims=True)

    def exchange(src, ring, count, send_sem, recv_sem, peer):
        def copy(j):
            return pltpu.make_async_remote_copy(
                src_ref=src,
                dst_ref=ring.at[j],
                send_sem=send_sem.at[j],
                recv_sem=recv_sem.at[j],
                device_id=peer(j),
                device_id_type=MESH,
            )

        @pl.loop(1, count)
        def _(j):
            copy(j).start()

        def finish():
            @pl.loop(1, count)
            def _(j):
                copy(j).wait()

        return finish

    def reduce_start(total, ring_a, recv_a):
        part_a[...] = total
        ring_a[0] = total
        return exchange(part_a, ring_a, 16, ar_send_a, recv_a, peer_a)

    def reduce_second(finish, ring_a, ring_b, recv_b):
        finish()
        total = jnp.sum(ring_a[...], axis=0)
        part_b[...] = total
        ring_b[0] = total
        return exchange(part_b, ring_b, 32, ar_send_b, recv_b, peer_b)

    def reduce_rate(finish, ring_b):
        finish()
        total = jnp.sum(jnp.sum(ring_b[...], axis=0), axis=1, keepdims=True)
        return jnp.broadcast_to(STEP_SCALE / jnp.sqrt(total / ENTRIES + EPS), (8, 128))

    columns(None)
    payoffs(ROWS_ALL)
    first = reduce_start(values_up(), ring_a1, ar_recv_a1)
    rate = reduce_rate(reduce_second(first, ring_a1, ring_b1, ar_recv_b1), ring_b1)
    columns(rate)
    payoffs(ROWS)
    first = reduce_start(values_up(), ring_a2, ar_recv_a2)

    def back(idx, src, dst, step):
        return pltpu.make_async_remote_copy(
            src_ref=src,
            dst_ref=dst,
            send_sem=ret_send.at[idx],
            recv_sem=ret_recv.at[idx],
            device_id=at_node(step),
            device_id_type=MESH,
        )

    backs = [
        back(0, qbuf.at[3], ret3a, 1),
        back(1, qbuf.at[3], ret3b, 2),
        back(2, qbuf.at[2], ret2, 1),
        back(3, qbuf.at[0], ret0, -1),
    ]
    for copy in backs:
        copy.start()
    second = reduce_second(first, ring_a2, ring_b2, ar_recv_b2)

    def scatter(level, shift, rows):
        count = rows.shape[0]
        out_row = iota((32, count), 0)
        col = iota((32, count), 1)
        same_slot = jnp.bitwise_and(out_row, 3) == jnp.bitwise_and(col // 8, 3)
        chain = 8 * (col // 32) + jnp.bitwise_and(col, 7)
        hit = jnp.logical_and(same_slot, chain == out_row // 4 + shift)
        fin_values[level] = pick_rows(hit, rows)[:, 0:HANDS]

    scatter(1, 0, qbuf[1])
    backs[3].wait()
    scatter(0, off1, jnp.concatenate([qbuf[0], ret0[...]], axis=0))
    backs[2].wait()
    scatter(2, 8 - off2, jnp.concatenate([ret2[...], qbuf[2]], axis=0))
    backs[0].wait()
    backs[1].wait()
    scatter(3, 16 - off23, jnp.concatenate([ret3b[...], ret3a[...], qbuf[3]], axis=0))
    write_values = pltpu.make_async_copy(fin_values, out_values.at[0], out_sem.at[0])
    write_values.start()
    rate = reduce_rate(second, ring_b2)
    for level in range(LEVELS):
        fin_logits[level] = own[level] + rate[0:1, 0:1] * fin_values[level]
    write_logits = pltpu.make_async_copy(fin_logits, out_logits.at[0], out_sem.at[1])
    write_logits.start()
    write_values.wait()
    write_logits.wait()


def per_device(
    logits, pot_size, node_type, parent_slot, range_one, range_two, hand_rank, live_mask
):
    small = (LEVELS, SLOT_DEV)
    rows = (SLOT_DEV, HANDS)
    wide = (SLOT_DEV, PAD)
    vmem = pltpu.VMEM
    dma = pltpu.SemaphoreType.DMA
    scratch = [
        vmem((LEVELS,) + rows, F32),
        vmem(small, F32),
        vmem(small, jnp.int32),
        pltpu.SMEM(small, jnp.int32),
        vmem((1, HANDS), F32),
        vmem((1, HANDS), F32),
        vmem((1, HANDS), jnp.int32),
        vmem((1, HANDS), jnp.int32),
        vmem((64, PAD), F32),
        vmem(rows, F32),
        vmem(rows, F32),
        vmem(rows, F32),
        vmem((24, HANDS), F32),
        vmem(small, F32),
        vmem(small, F32),
        vmem(small, F32),
        vmem(small, jnp.int32),
        vmem(small, jnp.int32),
        vmem(small, jnp.int32),
        vmem((1, PAD), F32),
        vmem((1, PAD), F32),
        vmem((1, PAD), F32),
        vmem((1, PAD), F32),
        vmem((64, PAD), BF16),
        vmem((64, PAD), BF16),
        vmem((3, LEVELS, 4, 8, 128), F32),
        vmem((LEVELS,) + wide, F32),
        vmem((2,) + wide, F32),
        vmem((LEVELS,) + wide, F32),
        vmem((ROWS_ALL, 2 * PAD), BF16),
        vmem((2 * PAD, PAD), BF16),
        vmem((ROWS_ALL, PAD), F32),
        vmem((1, 128), F32),
        vmem((1, 128), F32),
        vmem((16, 1, 128), F32),
        vmem((32, 1, 128), F32),
        vmem((16, 1, 128), F32),
        vmem((32, 1, 128), F32),
        vmem(wide, F32),
        vmem(wide, F32),
        vmem(wide, F32),
        vmem(wide, F32),
        vmem((LEVELS,) + rows, F32),
        vmem((LEVELS,) + rows, F32),
        dma((9,)),
        dma((2,)),
        dma((10,)),
        dma((10,)),
        dma((4,)),
        dma((4,)),
        dma((16,)),
        dma((32,)),
        dma((16,)),
        dma((32,)),
        dma((16,)),
        dma((32,)),
    ]
    whole = jax.ShapeDtypeStruct(logits.shape, F32)
    hbm = pl.BlockSpec(memory_space=pl.ANY)
    return pl.pallas_call(
        kernel,
        name="extragradient",
        out_shape=(whole, whole),
        in_specs=[hbm] * 9,
        out_specs=(hbm, hbm),
        scratch_shapes=scratch,
        compiler_params=pltpu.CompilerParams(
            collective_id=0, has_side_effects=True, vmem_limit_bytes=48 * 1024 * 1024
        ),
    )(
        logits,
        pot_size,
        node_type,
        parent_slot,
        range_one,
        range_two,
        hand_rank,
        live_mask,
        jnp.asarray(card_rows()),
    )


def solution(mesh):
    placed = (
        P("board", None, "node", None),
        P(None, "node"),
        P(None, "node"),
        P(None, "node"),
        P("board", None),
        P("board", None),
        P("board", None),
        P("board", None),
    )
    return jax.shard_map(
        per_device,
        mesh=mesh,
        in_specs=placed,
        out_specs=(P("board", None, "node", None), P("board", None, "node", None)),
        check_vma=False,
    )
```

time: 295 us -> 64.7 us (0.22); the launches traced: 290 us -> 64.2 us
  blocking collectives: 81.7 us -> 0 us
  starting transfers between devices: 68.5 us -> 0 us
  waiting for transfers between devices: 57.1 us -> 0 us
  Pallas kernels: 0 us -> 55 us
  matrix products: 30.2 us -> 0 us
  local copies, waits for them, and re-layouts: 28.8 us -> 8.61 us
  other arithmetic: 19.7 us -> 0 us
  between operations: 3.9 us -> 0.66 us
    psum x8 -> x0, blocking collectives: 81.7 us -> none  [one_axis_at_a_time(): return functools.reduce(lax.psum, axes, value)]
    ppermute x21 -> x0, starting transfers between devices: 68.5 us -> none  [passed_along(): return lax.ppermute(value, axis, pairs)]
    ppermute x21 -> x0, waiting for transfers between devices: 57.1 us -> none  [passed_along(): return lax.ppermute(value, axis, pairs)]
    pallas_call x0 -> x1, Pallas kernels: none -> 55 us  [per_device(): pl.pallas_call(kernel, name='extragradient', out_shape=(whole, whole), in...]
    dot_general x34 -> x0, matrix products: 30.2 us -> none  [the longest x2 7.3 us: terminal_pay(): jnp.einsum('bij,bnj->bni', show_block, show_cols, preferred_element_type=...]
    gather x22 -> x0, local copies, waits for them, and re-layouts: 14.6 us -> none  [the longest x6 4.17 us: reach_levels(): above_one = jnp.take(window_one, local_idx, axis=1)]
    unnamed x130 -> x20, local copies, waits for them, and re-layouts: 2.64 us -> 8.61 us
    slice x9 -> x0, local copies, waits for them, and re-layouts: 4.95 us -> none  [the longest x4 2.64 us: terminal_pay(): pay_one = product[:, :column_count].reshape(boards, LEVELS, SLOT_DEV, HANDS)]
  transfers between devices with their start and end apart: 21 -> 0, of which waited for: 12 -> 0; matrix products, arithmetic and copies ran while one was open for 10% -> 0% of each run, Pallas kernels for 0% -> 0%
where the time goes in v1:
time: 64.7 us; the launch traced here: 64.2 us
  Pallas kernels  55 us (85%)
  local copies, waits for them, and re-layouts  8.61 us (13%)
  between operations  0.66 us (1%)
    pallas_call x1, Pallas kernels, per_device(): pl.pallas_call(kernel, name='extragradient', out_shape=(whole, whole), in...  55 us
    unnamed x20, local copies, waits for them, and re-layouts  8.61 us

profile of v1, /device:TPU:1, one launch (start us, length us, event | category | flops | bytes accessed | tf_op | source)
XLA Modules:
  0.0 64.2 jit_solution(15407901916298359794)
XLA Ops:
  0.6 0.0 copy-start
  0.6 1.1 %copy-done = f32[1,4,32,1326]{3,2,1,0:T(8,128)S(1)} copy-done((f32[1,4,32,1326]{3,2,1,0:T(8,128)S(1)}, f32[1,4,32,1326]{3,2,1,0:T(8,128)}, u32[]{:S(2)}) %copy-start) | copy-done | bytes 678936
  1.7 0.0 copy-start.1
  1.7 1.0 %copy-done.1 = f32[64,1408]{1,0:T(8,128)S(1)} copy-done((f32[64,1408]{1,0:T(8,128)S(1)}, f32[64,1408]{1,0:T(8,128)}, u32[]{:S(2)}) %copy-start.1) | copy-done | bytes 360472
  2.7 0.0 copy-start.2
  2.7 0.7 %copy-done.2 = f32[1,1326]{1,0:T(1,128)S(1)} copy-done((f32[1,1326]{1,0:T(1,128)S(1)}, f32[1,1326]{1,0:T(1,128)}, u32[]{:S(2)}) %copy-start.2) | copy-done | bytes 5328
  3.4 0.0 copy-start.3
  3.4 0.7 %copy-done.3 = f32[1,1326]{1,0:T(1,128)S(1)} copy-done((f32[1,1326]{1,0:T(1,128)S(1)}, f32[1,1326]{1,0:T(1,128)}, u32[]{:S(2)}) %copy-start.3) | copy-done | bytes 5328
  4.1 0.0 copy-start.4
  4.1 0.7 %copy-done.4 = s32[1,1326]{1,0:T(1,128)S(1)} copy-done((s32[1,1326]{1,0:T(1,128)S(1)}, s32[1,1326]{1,0:T(1,128)}, u32[]{:S(2)}) %copy-start.4) | copy-done | bytes 5328
  4.8 0.0 copy-start.5
  4.8 0.7 %copy-done.5 = s32[1,1326]{1,0:T(1,128)S(1)} copy-done((s32[1,1326]{1,0:T(1,128)S(1)}, s32[1,1326]{1,0:T(1,128)}, u32[]{:S(2)}) %copy-start.5) | copy-done | bytes 5328
  5.5 0.0 copy-start.6
  5.5 0.7 %copy-done.6 = f32[4,32]{1,0:T(4,128)S(1)} copy-done((f32[4,32]{1,0:T(4,128)S(1)}, f32[4,32]{1,0:T(4,128)}, u32[]{:S(2)}) %copy-start.6) | copy-done | bytes 536
  6.2 0.0 copy-start.7
  6.2 0.7 %copy-done.7 = s32[4,32]{1,0:T(4,128)S(1)} copy-done((s32[4,32]{1,0:T(4,128)S(1)}, s32[4,32]{1,0:T(4,128)}, u32[]{:S(2)}) %copy-start.7) | copy-done | bytes 536
  6.9 0.0 copy-start.8
  6.9 0.7 %copy-done.8 = s32[4,32]{1,0:T(4,128)S(1)} copy-done((s32[4,32]{1,0:T(4,128)S(1)}, s32[4,32]{1,0:T(4,128)}, u32[]{:S(2)}) %copy-start.8) | copy-done | bytes 536
  7.5 55.0 %extragradient.1 = (f32[1,4,32,1326]{3,2,1,0:T(8,128)S(1)}, f32[1,4,32,1326]{3,2,1,0:T(8,128)S(1)}) custom-call(f32[1,4,32,1326]{3,2,1,0:T(8,128)S(1)} %copy-done, f32[4,32]{1,0:T(4,128)S(1)} %copy-done.6, s32[4,32]{1,0:T(4,128)S(1)} %copy-done.7, s32[4,32]{1,0:T(4,128)S(1)} %copy-done.8, f32[1,1326]{1,0:T(1,128)S(1)} %copy-done.2, f32[1,1326]{1,0:T(1,128)S(1)} %copy-done.3, ...), custom_call_target="tpu_custom_call" | custom-call | tf_op jit(solution)/shard_map/extragradient/pallas_call | solution.py:566
  62.5 0.9 %copy.13 = f32[1,4,32,1326]{3,2,1,0:T(8,128)} copy(f32[1,4,32,1326]{3,2,1,0:T(8,128)S(1)} %get-tuple-element.4) | data formatting | bytes 1357824
  63.4 0.9 %copy.14 = f32[1,4,32,1326]{3,2,1,0:T(8,128)} copy(f32[1,4,32,1326]{3,2,1,0:T(8,128)S(1)} %get-tuple-element.5) | data formatting | bytes 1357824
Async XLA Ops:
  0.6 1.1 %copy-start = (f32[1,4,32,1326]{3,2,1,0:T(8,128)S(1)}, f32[1,4,32,1326]{3,2,1,0:T(8,128)}, u32[]{:S(2)}) copy-start(f32[1,4,32,1326]{3,2,1,0:T(8,128)} %logits.1) | copy-start | bytes 2036740
  1.7 1.0 %copy-start.1 = (f32[64,1408]{1,0:T(8,128)S(1)}, f32[64,1408]{1,0:T(8,128)}, u32[]{:S(2)}) copy-start(f32[64,1408]{1,0:T(8,128)} %constant.2.clone.cards) | copy-start | bytes 1081348
  2.7 0.7 %copy-start.2 = (f32[1,1326]{1,0:T(1,128)S(1)}, f32[1,1326]{1,0:T(1,128)}, u32[]{:S(2)}) copy-start(f32[1,1326]{1,0:T(1,128)} %range_one.1) | copy-start | bytes 15916
  3.4 0.7 %copy-start.3 = (f32[1,1326]{1,0:T(1,128)S(1)}, f32[1,1326]{1,0:T(1,128)}, u32[]{:S(2)}) copy-start(f32[1,1326]{1,0:T(1,128)} %range_two.1) | copy-start | bytes 15916
  4.1 0.7 %copy-start.4 = (s32[1,1326]{1,0:T(1,128)S(1)}, s32[1,1326]{1,0:T(1,128)}, u32[]{:S(2)}) copy-start(s32[1,1326]{1,0:T(1,128)} %rank.1) | copy-start | bytes 15916
  4.8 0.7 %copy-start.5 = (s32[1,1326]{1,0:T(1,128)S(1)}, s32[1,1326]{1,0:T(1,128)}, u32[]{:S(2)}) copy-start(s32[1,1326]{1,0:T(1,128)} %live.1) | copy-start | bytes 15916
  5.5 0.7 %copy-start.6 = (f32[4,32]{1,0:T(4,128)S(1)}, f32[4,32]{1,0:T(4,128)}, u32[]{:S(2)}) copy-start(f32[4,32]{1,0:T(4,128)} %pot.1) | copy-start | bytes 1540
  6.2 0.7 %copy-start.7 = (s32[4,32]{1,0:T(4,128)S(1)}, s32[4,32]{1,0:T(4,128)}, u32[]{:S(2)}) copy-start(s32[4,32]{1,0:T(4,128)} %kind.1) | copy-start | bytes 1540
  6.9 0.7 %copy-start.8 = (s32[4,32]{1,0:T(4,128)S(1)}, s32[4,32]{1,0:T(4,128)}, u32[]{:S(2)}) copy-start(s32[4,32]{1,0:T(4,128)} %parent.1) | copy-start | bytes 1540

commit v2 on v1

v2 whole, which is shorter than its diff:
```python
import functools

import jax
import jax.numpy as jnp
import numpy as np
from jax import lax
from jax.experimental import pallas as pl
from jax.experimental.pallas import tpu as pltpu
from jax.sharding import PartitionSpec as P

HANDS = 1326
PAD = 1408
CHUNKS = PAD // 128
LEVELS = 4
SLOT_DEV = 32
GROUPS = SLOT_DEV // 4
NODES = 64
BOARDS = 8
ALL_GROUPS = NODES * GROUPS
ENTRIES = BOARDS * LEVELS * NODES * SLOT_DEV * HANDS
STEP_SCALE = 0.5
EPS = 1e-06
CHIPS = NODES // 2
PEERS_A = 2 * BOARDS
ROW1, ROW2, ROW3, ROWS = 32, 80, 128, 176
F32 = jnp.float32
BF16 = jnp.bfloat16
MESH = pl.DeviceIdType.MESH


KEEP_A = 4
CARDS = 52
DEEP = PAD + 3 * 64


def card_rows():
    table = np.zeros((64, PAD), np.float32)
    hand = 0
    for low in range(52):
        for high in range(low + 1, 52):
            if hand < HANDS:
                table[low, hand] = 1.0
                table[high, hand] = 1.0
                hand += 1
    return table


def iota(shape, dim):
    return lax.broadcasted_iota(jnp.int32, shape, dim)


def three_parts(value):
    high = value.astype(BF16)
    rest = value - high.astype(F32)
    mid = rest.astype(BF16)
    return [high, mid, (rest - mid.astype(F32)).astype(BF16)]


def pick_rows(pick, rows):
    parts = jnp.concatenate(three_parts(rows), axis=0)
    pick = jnp.concatenate([pick, pick, pick], axis=1).astype(BF16)
    return jnp.dot(pick, parts, preferred_element_type=F32)


def third(value):
    return jnp.right_shift(value * 43, 7)


def kernel(
    logits,
    pot,
    kind,
    parent,
    range_one,
    range_two,
    rank,
    live,
    cards,
    cards_t,
    out_logits,
    out_values,
    own,
    own_pot,
    own_kind,
    parent_s,
    rng1,
    rng2,
    rank_v,
    live_v,
    cards_v,
    cards_tv,
    diffs,
    win0a,
    win0b,
    win1,
    win2,
    win3a,
    win3b,
    near_pot,
    near_kind,
    reach1,
    reach2,
    rank_p,
    dead_p,
    rhs_cards,
    table,
    zbuf,
    strat,
    qbuf,
    qsend,
    cols,
    folds,
    blocks,
    pay,
    part_a,
    part_b,
    ring_a1,
    ring_b1,
    ring_a2,
    ring_b2,
    ret0a,
    ret0b,
    ret1,
    ret2,
    ret3a,
    ret3b,
    hold,
    known,
    in_sem,
    halo_send,
    halo_recv,
    ret_send,
    ret_recv,
    ar_send_a,
    ar_send_b,
    ar_recv_a1,
    ar_recv_b1,
    ar_recv_a2,
    ar_recv_b2,
):
    node = lax.axis_index("node")
    board = lax.axis_index("board")
    core = lax.rem(node, 2)
    chip = node // 2

    def at_node(step):
        return {"node": lax.rem(node + step + NODES, NODES), "board": board}

    def at_board(step):
        return {"node": node, "board": lax.rem(board + step + BOARDS, BOARDS)}

    def peer_a(j):
        spot = lax.rem(board * 2 + core + j, PEERS_A)
        return {"node": chip * 2 + lax.rem(spot, 2), "board": spot // 2}

    def peer_b(j):
        return {"node": lax.rem(chip + j, CHIPS) * 2 + core, "board": board}

    loads = [
        pltpu.make_async_copy(src, dst, in_sem.at[idx])
        for idx, (src, dst) in enumerate(
            [
                (live, live_v),
                (rank, rank_v),
                (cards, cards_v),
                (cards_t, cards_tv),
                (pot, own_pot),
                (kind, own_kind),
                (parent, parent_s),
                (range_one, rng1),
                (range_two, rng2),
                (logits.at[0], own),
            ]
        )
    ]

    barrier = pltpu.get_barrier_semaphore()
    close = [at_node(step) for step in (1, -1, 2, -2)]
    if BOARDS > 1:
        close += [at_board(step) for step in (1, -1)]
    for peer in close:
        pl.semaphore_signal(barrier, inc=1, device_id=peer, device_id_type=MESH)
    for load in loads:
        load.start()
    rounds = []
    step = 1
    while step < CHIPS // 2 or step <= BOARDS // 2:
        peers = []
        if step < CHIPS // 2:
            peers += [at_node(2 * step), at_node(-2 * step)]
        if step < BOARDS // 2:
            peers += [at_board(step), at_board(-step)]
        elif step == BOARDS // 2:
            peers += [at_board(step)]
        rounds.append(peers)
        step *= 2

    def announce(idx):
        if idx < len(rounds):
            for peer in rounds[idx]:
                pl.semaphore_signal(known.at[idx], inc=1, device_id=peer, device_id_type=MESH)

    def heard(idx):
        if idx < len(rounds):
            pl.semaphore_wait(known.at[idx], len(rounds[idx]))

    def halo(idx, src, dst, step):
        return pltpu.make_async_remote_copy(
            src_ref=src,
            dst_ref=dst,
            send_sem=halo_send.at[idx],
            recv_sem=halo_recv.at[idx],
            device_id=at_node(step),
            device_id_type=MESH,
        )

    halos = []
    for spot, step in enumerate((1, -1, 2, -2)):
        halos.append(halo(2 * spot, pot, near_pot.at[spot], step))
        halos.append(halo(2 * spot + 1, kind, near_kind.at[spot], step))
    sends = [
        halo(8, diffs.at[1, pl.ds(0, 16)], win1, 1),
        halo(9, diffs.at[0], win0a, 1),
        halo(10, diffs.at[0, pl.ds(0, 16)], win0b, 2),
        halo(11, diffs.at[2, pl.ds(0, 16)], win2, -1),
        halo(12, diffs.at[3], win3a, -1),
        halo(13, diffs.at[3, pl.ds(0, 8)], win3b, -2),
    ]
    pl.semaphore_wait(barrier, len(close))
    for copy in halos:
        copy.start()
    announce(0)
    loads[-1].wait()

    out_row = iota((24, SLOT_DEV), 0)
    col = iota((24, SLOT_DEV), 1)
    for level, copies in ((1, sends[0:1]), (0, sends[1:3]), (2, sends[3:4]), (3, sends[4:6])):
        group = third(out_row)
        slot = out_row - 3 * group + 1
        group = GROUPS - 1 - group if level < 2 else group
        pick = jnp.where(col == 4 * group + slot, 1.0, jnp.where(col == 4 * group, -1.0, 0.0))
        diffs[level, :, 0:HANDS] = pick_rows(pick, own[level])
        diffs[level, :, HANDS:PAD] = jnp.zeros((24, PAD - HANDS), F32)
        for copy in copies:
            copy.start()
    for load in loads[:-1]:
        load.wait()

    zero_row = jnp.zeros((1, PAD), F32)
    reach1[...] = zero_row
    reach2[...] = zero_row
    rank_p[...] = zero_row
    alive = jnp.where(live_v[...] > 0, 1.0, 0.0)
    reach1[:, 0:HANDS] = rng1[...] * alive
    reach2[:, 0:HANDS] = rng2[...] * alive
    rank_p[:, 0:HANDS] = rank_v[...].astype(F32)
    dead_p[...] = jnp.ones((1, PAD), F32)
    dead_p[:, 0:HANDS] = 1.0 - alive
    dead = dead_p[...]
    row = iota((16, PAD), 0)
    head = cards_v[0:48]
    tail = cards_v[48:64]
    rhs_cards[0:48] = head.astype(BF16)
    rhs_cards[48:64] = jnp.where(row == CARDS - 48, dead, tail).astype(BF16)
    lively = 1.0 - dead
    for part in range(3):
        top = PAD + 64 * part
        blocks[top : top + 48] = (-head * lively).astype(BF16)
        blocks[top + 48 : top + 64] = jnp.where(row == CARDS - 48, lively, -tail * lively).astype(BF16)

    @pl.loop(0, CHUNKS)
    def _(jb):
        base = pl.multiple_of(jb * 128, 128)
        rank_j = jnp.broadcast_to(rank_p[:, pl.ds(base, 128)], (128, 128)).T
        mine = cards_tv[pl.ds(base, 128)]
        for first in range(0, PAD, 256):
            last = min(first + 256, PAD)
            shared = jnp.dot(mine, rhs_cards[:, first:last], preferred_element_type=F32)
            for start in range(first, last, 128):
                span = slice(start, start + 128)
                keep = shared[:, start - first : start - first + 128] < 0.5
                order = jnp.clip(rank_p[:, span] - rank_j, -1.0, 1.0)
                blocks[pl.ds(base, 128), span] = jnp.where(keep, order, 0.0).astype(BF16)

    def offset(level):
        return jnp.bitwise_and(node * GROUPS - parent_s[level, 0] // 4 + ALL_GROUPS, ALL_GROUPS - 1)

    off1 = offset(1)
    off2 = offset(2)
    off3 = offset(3)

    def places(chain):
        late = jnp.logical_and(chain >= KEEP_A, chain + off2 >= GROUPS)
        first = jnp.where(late, chain - GROUPS, chain)
        return [first - off1, first, first + off2, first + off2 + off3]

    heard(0)
    announce(1)
    for copy in halos:
        copy.wait()

    lane = iota((8, SLOT_DEV), 1)
    spots = places(iota((8, SLOT_DEV), 0))
    near = {1: 1, -1: 0, 2: 3, -2: 2}

    def fill_table(level, steps):
        for k in range(4):
            pots = jnp.zeros((8, SLOT_DEV), F32)
            kinds = jnp.zeros((8, SLOT_DEV), F32)
            for step in steps:
                pot_row = own_pot[level : level + 1] if step == 0 else near_pot[near[step], level : level + 1]
                kind_row = own_kind[level : level + 1] if step == 0 else near_kind[near[step], level : level + 1]
                hit = lane + SLOT_DEV * step == 4 * spots[level] + k
                pots += jnp.where(hit, pot_row, 0.0)
                kinds += jnp.where(hit, kind_row.astype(F32), 0.0)
            pots = jnp.broadcast_to(jnp.sum(pots, axis=1, keepdims=True), (8, 128))
            kinds = jnp.broadcast_to(jnp.sum(kinds, axis=1, keepdims=True), (8, 128))
            sign = -1.0 if level % 2 == 0 else 1.0
            table[0, level, k] = jnp.where(kinds > 1.5, pots, 0.0)
            table[1, level, k] = jnp.where(jnp.abs(kinds - 1.0) < 0.5, pots, 0.0) * sign
            table[2, level, k] = jnp.where(kinds < 0.5, 1.0, 0.0)

    fill_table(0, (-2, -1, 0))
    fill_table(1, (-1, 0))
    fill_table(2, (0, 1))
    fill_table(3, (0, 1, 2))

    def gather(level, windows):
        rows = jnp.concatenate([ref[...] for _, ref in windows], axis=0)
        pick = []
        for step, ref in windows:
            shape = (24, ref.shape[0])
            out_row = iota(shape, 0)
            spot = places(jnp.bitwise_and(out_row, 7))[level] - GROUPS * step
            spot = GROUPS - 1 - spot if level < 2 else spot
            inside = jnp.logical_and(spot >= 0, spot < GROUPS)
            want = 3 * spot + jnp.right_shift(out_row, 3)
            hit = jnp.logical_and(inside, iota(shape, 1) == want)
            pick.append(jnp.where(hit, 1.0, 0.0))
        zbuf[level] = pick_rows(jnp.concatenate(pick, axis=1), rows)

    def put(first_row, span, fold, even, odd):
        pair = jnp.concatenate([even, odd], axis=0).astype(BF16)
        target = folds if fold else cols
        target[first_row : first_row + 16, pl.ds(span, 128)] = pair

    def rounded(value):
        return value.astype(BF16).astype(F32)

    def put_sum(first_row, span, fold, value):
        high = rounded(value)
        put(first_row, span, fold, high, value - high)

    def columns(rate, levels):
        @pl.loop(0, CHUNKS)
        def _(chunk):
            span = pl.multiple_of(chunk * 128, 128)

            def soft(level):
                z = [zbuf[level, 8 * k : 8 * k + 8, pl.ds(span, 128)] for k in range(3)]
                if rate is not None:
                    q = [qbuf[level, 8 * k : 8 * k + 8, pl.ds(span, 128)] for k in range(4)]
                    z = [z[k] + rate * (q[k + 1] - q[0]) for k in range(3)]
                z = [jnp.zeros((8, 128), F32)] + z
                top = jnp.maximum(jnp.maximum(z[0], z[1]), jnp.maximum(z[2], z[3]))
                e = [jnp.exp(x - top) for x in z]
                inv = 1.0 / ((e[0] + e[1]) + (e[2] + e[3]))
                return [x * inv for x in e]

            def inner(level, values):
                return sum(table[2, level, k] * values[k] for k in range(4))

            def both(level, values, sign):
                show = [values[k] * table[0, level, k] for k in range(4)]
                fold = [values[k] * table[1, level, k] for k in range(4)]
                return show, [-x for x in fold] if sign < 0 else fold

            def put_slots(first_row, pairs):
                for fold, values in enumerate(pairs):
                    put(first_row, span, fold, values[0], values[1])
                    put(first_row + 16, span, fold, values[2], values[3])

            def put_sums(first_row, pairs):
                for fold, values in enumerate(pairs):
                    put_sum(first_row, span, fold, sum(rounded(x) for x in values))

            one = reach1[:, pl.ds(span, 128)]
            two = reach2[:, pl.ds(span, 128)]
            if 0 in levels and rate is None:
                put_slots(0, both(0, [two] * 4, 1))
            if 0 in levels:
                x1 = one * inner(0, soft(0))
                y1 = [two * s for s in soft(1)]
                y2 = inner(1, y1)
                put_slots(ROW1, both(1, [x1] * 4, -1))
                put_sums(ROW1 + 32, both(1, y1, 1))
                s2 = soft(2)
                x2 = [x1 * s for s in s2]
                x3 = inner(2, x2)
                put_slots(ROW2, both(2, [y2] * 4, 1))
                put_sums(ROW2 + 32, both(2, x2, -1))
                for k in range(4):
                    strat[0, 8 * k : 8 * k + 8, pl.ds(span, 128)] = s2[k]
            if 3 not in levels:
                hold[0, :, pl.ds(span, 128)] = x3
                hold[1, :, pl.ds(span, 128)] = y2
                return
            if 0 not in levels:
                x3 = hold[0, :, pl.ds(span, 128)]
                y2 = hold[1, :, pl.ds(span, 128)]
            s3 = soft(3)
            y3 = [y2 * s for s in s3]
            put_slots(ROW3, both(3, [x3] * 4, -1))
            put_sums(ROW3 + 32, both(3, y3, 1))
            for k in range(4):
                strat[1, 8 * k : 8 * k + 8, pl.ds(span, 128)] = s3[k]

    def payoffs(top, end):
        sums = jnp.dot(folds[top:end, :], cards_tv[...], preferred_element_type=F32)
        for part, value in enumerate(three_parts(sums)):
            cols[top:end, PAD + 64 * part : PAD + 64 * part + 64] = value
        for first in range(0, PAD, 256):
            last = min(first + 256, PAD)
            pay[top:end, first:last] = jnp.dot(
                cols[top:end, :], blocks[:, first:last], preferred_element_type=F32
            )

    def values_up(last):
        def step(chunk, total):
            span = pl.multiple_of(chunk * 128, 128)
            lively = 1.0 - dead_p[:, pl.ds(span, 128)]

            def pair(first_row):
                fold = folds[first_row : first_row + 16, pl.ds(span, 128)].astype(F32)
                both = pay[first_row : first_row + 16, pl.ds(span, 128)] + fold * lively
                return [both[0:8], both[8:16]]

            def slots(first_row):
                return pair(first_row) + pair(first_row + 16)

            def summed(first_row):
                return sum(pair(first_row))

            def weighted(which, values):
                return sum(
                    strat[which, 8 * k : 8 * k + 8, pl.ds(span, 128)] * values[k]
                    for k in range(4)
                )

            def joined(level, values, below):
                return [values[k] + table[2, level, k] * below for k in range(4)]

            q3 = slots(ROW3)
            q2 = joined(2, slots(ROW2), summed(ROW3 + 32))
            q1 = joined(1, slots(ROW1), summed(ROW2 + 32) + weighted(1, q3))
            q0 = joined(0, slots(0), summed(ROW1 + 32) + weighted(0, q2))
            for level, q in enumerate((q0, q1, q2, q3)):
                if last:
                    for k in (0, 2):
                        for half in (0, 4):
                            rows = jnp.concatenate([q[k][half : half + 4], q[k + 1][half : half + 4]], axis=0)
                            top = 4 * half + 4 * k
                            qsend[level, top : top + 8, pl.ds(span, 128)] = rows
                else:
                    for k in range(4):
                        qbuf[level, 8 * k : 8 * k + 8, pl.ds(span, 128)] = q[k]
                total = total + ((q[0] * q[0] + q[1] * q[1]) + (q[2] * q[2] + q[3] * q[3]))
            return total

        total = lax.fori_loop(0, CHUNKS, step, jnp.zeros((8, 128), F32))
        return jnp.sum(total, axis=0, keepdims=True)

    def exchange(src, ring, count, send_sem, recv_sem, peer):
        def copy(j):
            return pltpu.make_async_remote_copy(
                src_ref=src,
                dst_ref=ring.at[j],
                send_sem=send_sem.at[j],
                recv_sem=recv_sem.at[j],
                device_id=peer(j),
                device_id_type=MESH,
            )

        copies = [copy(j) for j in sorted(range(1, count), key=lambda j: -min(j, count - j))]
        for item in copies:
            item.start()

        def finish():
            for item in reversed(copies):
                item.wait()

        return finish

    def reduce_start(total, ring_a, recv_a):
        part_a[...] = total
        ring_a[0] = total
        return exchange(part_a, ring_a, PEERS_A, ar_send_a, recv_a, peer_a)

    def reduce_second(finish, ring_a, ring_b, recv_b):
        finish()
        total = jnp.sum(ring_a[...], axis=0)
        part_b[...] = total
        ring_b[0] = total
        return exchange(part_b, ring_b, CHIPS, ar_send_b, recv_b, peer_b)

    def reduce_rate(finish, ring_b):
        finish()
        total = jnp.sum(jnp.sum(ring_b[...], axis=0), axis=1, keepdims=True)
        return jnp.broadcast_to(STEP_SCALE / jnp.sqrt(total / ENTRIES + EPS), (8, 128))

    sends[0].wait()
    gather(1, [(0, diffs.at[1]), (-1, win1)])
    sends[1].wait()
    sends[2].wait()
    gather(0, [(0, diffs.at[0]), (-1, win0a), (-2, win0b)])
    heard(1)
    announce(2)
    sends[3].wait()
    gather(2, [(0, diffs.at[2]), (1, win2)])
    columns(None, (0, 1, 2))
    heard(2)
    announce(3)
    payoffs(0, ROW3)
    sends[4].wait()
    sends[5].wait()
    gather(3, [(0, diffs.at[3]), (1, win3a), (2, win3b)])
    columns(None, (3,))
    payoffs(ROW3, ROWS)
    heard(3)
    first = reduce_start(values_up(False), ring_a1, ar_recv_a1)
    rate = reduce_rate(reduce_second(first, ring_a1, ring_b1, ar_recv_b1), ring_b1)
    columns(rate, (0, 1, 2, 3))
    payoffs(ROW1, ROWS)
    first = reduce_start(values_up(True), ring_a2, ar_recv_a2)

    def back(idx, src, dst, step):
        return pltpu.make_async_remote_copy(
            src_ref=src,
            dst_ref=dst,
            send_sem=ret_send.at[idx],
            recv_sem=ret_recv.at[idx],
            device_id=at_node(step),
            device_id_type=MESH,
        )

    backs = [
        back(0, qsend.at[3], ret3a, 1),
        back(1, qsend.at[3, pl.ds(0, 16)], ret3b, 2),
        back(2, qsend.at[2, pl.ds(0, 16)], ret2, 1),
        back(3, qsend.at[0], ret0a, -1),
        back(4, qsend.at[0, pl.ds(16, 16)], ret0b, -2),
        back(5, qsend.at[1, pl.ds(16, 16)], ret1, -1),
    ]
    for copy in backs:
        copy.start()
    second = reduce_second(first, ring_a2, ring_b2, ar_recv_b2)

    def scatter(level, windows):
        rows = jnp.concatenate([ref[...] for _, _, ref in windows], axis=0)
        pick = []
        for step, half, ref in windows:
            shape = (SLOT_DEV, ref.shape[0])
            out_row = iota(shape, 0)
            col = iota(shape, 1) + 16 * half
            chain = 4 * jnp.right_shift(col, 4) + jnp.bitwise_and(col, 3)
            same_slot = jnp.bitwise_and(jnp.right_shift(col, 2), 3) == jnp.bitwise_and(out_row, 3)
            spot = places(chain)[level] + GROUPS * step
            hit = jnp.logical_and(same_slot, spot == jnp.right_shift(out_row, 2))
            pick.append(jnp.where(hit, 1.0, 0.0))
        out_values[0, level] = pick_rows(jnp.concatenate(pick, axis=1), rows)[:, 0:HANDS]

    backs[5].wait()
    scatter(1, [(0, 0, qsend.at[1]), (1, 1, ret1)])
    backs[3].wait()
    backs[4].wait()
    scatter(0, [(0, 0, qsend.at[0]), (1, 0, ret0a), (2, 1, ret0b)])
    backs[2].wait()
    scatter(2, [(0, 0, qsend.at[2]), (-1, 0, ret2)])
    backs[0].wait()
    backs[1].wait()
    scatter(3, [(0, 0, qsend.at[3]), (-1, 0, ret3a), (-2, 0, ret3b)])
    rate = reduce_rate(second, ring_b2)
    for level in range(LEVELS):
        out_logits[0, level] = own[level] + rate[0:1, 0:1] * out_values[0, level]


def per_device(
    logits, pot_size, node_type, parent_slot, range_one, range_two, hand_rank, live_mask
):
    small = (LEVELS, SLOT_DEV)
    rows = (SLOT_DEV, HANDS)
    wide = (SLOT_DEV, PAD)
    vmem = pltpu.VMEM
    dma = pltpu.SemaphoreType.DMA
    scratch = [
        vmem((LEVELS,) + rows, F32),
        vmem(small, F32),
        vmem(small, jnp.int32),
        pltpu.SMEM(small, jnp.int32),
        vmem((1, HANDS), F32),
        vmem((1, HANDS), F32),
        vmem((1, HANDS), jnp.int32),
        vmem((1, HANDS), jnp.int32),
        vmem((64, PAD), F32),
        vmem((PAD, 64), BF16),
        vmem((LEVELS, 24, PAD), F32),
        vmem((24, PAD), F32),
        vmem((16, PAD), F32),
        vmem((16, PAD), F32),
        vmem((16, PAD), F32),
        vmem((24, PAD), F32),
        vmem((8, PAD), F32),
        vmem((4,) + small, F32),
        vmem((4,) + small, jnp.int32),
        vmem((1, PAD), F32),
        vmem((1, PAD), F32),
        vmem((1, PAD), F32),
        vmem((1, PAD), F32),
        vmem((64, PAD), BF16),
        vmem((3, LEVELS, 4, 8, 128), F32),
        vmem((LEVELS, 24, PAD), F32),
        vmem((2,) + wide, F32),
        vmem((LEVELS,) + wide, F32),
        vmem((LEVELS,) + wide, F32),
        vmem((ROWS, DEEP), BF16),
        vmem((ROWS, PAD), BF16),
        vmem((DEEP, PAD), BF16),
        vmem((ROWS, PAD), F32),
        vmem((1, 128), F32),
        vmem((1, 128), F32),
        vmem((PEERS_A, 1, 128), F32),
        vmem((CHIPS, 1, 128), F32),
        vmem((PEERS_A, 1, 128), F32),
        vmem((CHIPS, 1, 128), F32),
        vmem(wide, F32),
        vmem((16, PAD), F32),
        vmem((16, PAD), F32),
        vmem((16, PAD), F32),
        vmem(wide, F32),
        vmem((16, PAD), F32),
        vmem((2, 8, PAD), F32),
        pltpu.SemaphoreType.REGULAR((4,)),
        dma((10,)),
        dma((14,)),
        dma((14,)),
        dma((6,)),
        dma((6,)),
        dma((PEERS_A,)),
        dma((CHIPS,)),
        dma((PEERS_A,)),
        dma((CHIPS,)),
        dma((PEERS_A,)),
        dma((CHIPS,)),
    ]
    whole = jax.ShapeDtypeStruct(logits.shape, F32)
    free = pl.BlockSpec(memory_space=pl.ANY)
    table = card_rows()
    turned = table.T.copy()
    turned[:, CARDS] = 1.0
    return pl.pallas_call(
        kernel,
        name="extragradient",
        out_shape=(whole, whole),
        in_specs=[free] * 10,
        out_specs=(pl.BlockSpec(memory_space=pltpu.VMEM),) * 2,
        scratch_shapes=scratch,
        compiler_params=pltpu.CompilerParams(
            collective_id=0, has_side_effects=True, vmem_limit_bytes=40 * 1024 * 1024
        ),
    )(
        *[
            pltpu.with_memory_space_constraint(value, pltpu.HBM)
            for value in (
                logits,
                pot_size,
                node_type,
                parent_slot,
                range_one,
                range_two,
                hand_rank,
                live_mask,
                jnp.asarray(table),
                jnp.asarray(turned, BF16),
            )
        ]
    )


def solution(mesh):
    placed = (
        P("board", None, "node", None),
        P(None, "node"),
        P(None, "node"),
        P(None, "node"),
        P("board", None),
        P("board", None),
        P("board", None),
        P("board", None),
    )
    return jax.shard_map(
        per_device,
        mesh=mesh,
        in_specs=placed,
        out_specs=(P("board", None, "node", None), P("board", None, "node", None)),
        check_vma=False,
    )
```

time: 64.7 us -> 52.5 us (0.81)
  local copies, waits for them, and re-layouts: 8.61 us -> 1.72 us
  Pallas kernels: 55 us -> 50 us
    unnamed x20 -> x2, local copies, waits for them, and re-layouts: 8.61 us -> 1.72 us
    pallas_call x1, Pallas kernels: 55 us -> 50 us  [per_device(): pl.pallas_call(kernel, name='extragradient', out_shape=(whole, whole), in...]
where the time goes in v2:
time: 52.5 us; the launch traced here: 52.3 us
  Pallas kernels  50 us (95%)
  local copies, waits for them, and re-layouts  1.72 us (3%)
  between operations  0.64 us (1%)
    pallas_call x1, Pallas kernels, per_device(): pl.pallas_call(kernel, name='extragradient', out_shape=(whole, whole), in...  50 us
    unnamed x2, local copies, waits for them, and re-layouts  1.72 us

profile of v2, /device:TPU:1, one launch (start us, length us, event | category | flops | bytes accessed | tf_op | source)
XLA Modules:
  0.0 52.3 jit_solution(6192866137685119134)
XLA Ops:
  0.6 50.0 %extragradient.1 = (f32[1,4,32,1326]{3,2,1,0:T(8,128)S(1)}, f32[1,4,32,1326]{3,2,1,0:T(8,128)S(1)}) custom-call(f32[1,4,32,1326]{3,2,1,0:T(8,128)} %logits.1, f32[4,32]{1,0:T(4,128)} %pot.1, s32[4,32]{1,0:T(4,128)} %kind.1, s32[4,32]{1,0:T(4,128)} %parent.1, f32[1,1326]{1,0:T(1,128)} %range_one.1, f32[1,1326]{1,0:T(1,128)} %range_two.1, s32[1,1326]{1,0:T(1,128)} %rank.1, ...), custom_call_target="tpu_custom_call" | custom-call | tf_op jit(solution)/shard_map/extragradient/pallas_call | solution.py:660
  50.6 0.9 %copy.14 = f32[1,4,32,1326]{3,2,1,0:T(8,128)} copy(f32[1,4,32,1326]{3,2,1,0:T(8,128)S(1)} %get-tuple-element.4) | data formatting | bytes 1357824
  51.5 0.9 %copy.15 = f32[1,4,32,1326]{3,2,1,0:T(8,128)} copy(f32[1,4,32,1326]{3,2,1,0:T(8,128)S(1)} %get-tuple-element.5) | data formatting | bytes 1357824

commit v3 on v2

--- a/solution.py
+++ b/solution.py
@@ -22,13 +22,13 @@
 EPS = 1e-06
 CHIPS = NODES // 2
 PEERS_A = 2 * BOARDS
-ROW1, ROW2, ROW3, ROWS = 32, 80, 128, 176
+ROW0, SUM1, ROW2, ROW1, SUM2, ROW3, SUM3, ROWS = 0, 32, 48, 80, 112, 128, 160, 176
 F32 = jnp.float32
 BF16 = jnp.bfloat16
 MESH = pl.DeviceIdType.MESH
 
 
-KEEP_A = 4
+KEEP_A = 5
 CARDS = 52
 DEEP = PAD + 3 * 64
 
@@ -125,7 +125,8 @@
     ret3a,
     ret3b,
     hold,
-    known,
+    known_node,
+    known_board,
     in_sem,
     halo_send,
     halo_recv,
@@ -160,6 +161,7 @@
         pltpu.make_async_copy(src, dst, in_sem.at[idx])
         for idx, (src, dst) in enumerate(
             [
+                (logits.at[0], own),
                 (live, live_v),
                 (rank, rank_v),
                 (cards, cards_v),
@@ -169,7 +171,6 @@
                 (parent, parent_s),
                 (range_one, rng1),
                 (range_two, rng2),
-                (logits.at[0], own),
             ]
         )
     ]
@@ -178,31 +179,36 @@
     close = [at_node(step) for step in (1, -1, 2, -2)]
     if BOARDS > 1:
         close += [at_board(step) for step in (1, -1)]
+    loads[0].start()
     for peer in close:
         pl.semaphore_signal(barrier, inc=1, device_id=peer, device_id_type=MESH)
-    for load in loads:
+    for load in loads[1:]:
         load.start()
-    rounds = []
+    along_node = []
     step = 1
-    while step < CHIPS // 2 or step <= BOARDS // 2:
-        peers = []
-        if step < CHIPS // 2:
-            peers += [at_node(2 * step), at_node(-2 * step)]
-        if step < BOARDS // 2:
-            peers += [at_board(step), at_board(-step)]
-        elif step == BOARDS // 2:
-            peers += [at_board(step)]
-        rounds.append(peers)
+    while step < CHIPS // 2:
+        along_node.append([at_node(2 * step), at_node(-2 * step)])
         step *= 2
-
-    def announce(idx):
+    along_board = []
+    step = 1
+    while step <= BOARDS // 2:
+        along_board.append([at_board(step), at_board(-step)][: 1 if 2 * step == BOARDS else 2])
+        step *= 2
+
+    def announce(idx, rounds, known):
         if idx < len(rounds):
             for peer in rounds[idx]:
                 pl.semaphore_signal(known.at[idx], inc=1, device_id=peer, device_id_type=MESH)
 
-    def heard(idx):
+    def heard(idx, rounds, known):
         if idx < len(rounds):
             pl.semaphore_wait(known.at[idx], len(rounds[idx]))
+
+    def next_round(idx):
+        heard(idx, along_node, known_node)
+        heard(idx, along_board, known_board)
+        announce(idx + 1, along_node, known_node)
+        announce(idx + 1, along_board, known_board)
 
     def halo(idx, src, dst, step):
         return pltpu.make_async_remote_copy(
@@ -221,29 +227,28 @@
     sends = [
         halo(8, diffs.at[1, pl.ds(0, 16)], win1, 1),
         halo(9, diffs.at[0], win0a, 1),
-        halo(10, diffs.at[0, pl.ds(0, 16)], win0b, 2),
+        halo(10, diffs.at[0, pl.ds(0, 8)], win0b, 2),
         halo(11, diffs.at[2, pl.ds(0, 16)], win2, -1),
         halo(12, diffs.at[3], win3a, -1),
-        halo(13, diffs.at[3, pl.ds(0, 8)], win3b, -2),
+        halo(13, diffs.at[3, pl.ds(0, 16)], win3b, -2),
     ]
-    pl.semaphore_wait(barrier, len(close))
-    for copy in halos:
-        copy.start()
-    announce(0)
-    loads[-1].wait()
+    loads[0].wait()
 
     out_row = iota((24, SLOT_DEV), 0)
     col = iota((24, SLOT_DEV), 1)
-    for level, copies in ((1, sends[0:1]), (0, sends[1:3]), (2, sends[3:4]), (3, sends[4:6])):
+    for level in range(LEVELS):
         group = third(out_row)
         slot = out_row - 3 * group + 1
         group = GROUPS - 1 - group if level < 2 else group
         pick = jnp.where(col == 4 * group + slot, 1.0, jnp.where(col == 4 * group, -1.0, 0.0))
         diffs[level, :, 0:HANDS] = pick_rows(pick, own[level])
         diffs[level, :, HANDS:PAD] = jnp.zeros((24, PAD - HANDS), F32)
-        for copy in copies:
-            copy.start()
-    for load in loads[:-1]:
+    pl.semaphore_wait(barrier, len(close))
+    for copy in halos + sends:
+        copy.start()
+    announce(0, along_node, known_node)
+    announce(0, along_board, known_board)
+    for load in loads[1:]:
         load.wait()
 
     zero_row = jnp.zeros((1, PAD), F32)
@@ -289,13 +294,13 @@
     off2 = offset(2)
     off3 = offset(3)
 
-    def places(chain):
+    def places(spot):
+        chain = jnp.bitwise_and(spot + 1, GROUPS - 1)
         late = jnp.logical_and(chain >= KEEP_A, chain + off2 >= GROUPS)
         first = jnp.where(late, chain - GROUPS, chain)
         return [first - off1, first, first + off2, first + off2 + off3]
 
-    heard(0)
-    announce(1)
+    next_round(0)
     for copy in halos:
         copy.wait()
 
@@ -351,7 +356,7 @@
         high = rounded(value)
         put(first_row, span, fold, high, value - high)
 
-    def columns(rate, levels):
+    def columns(rate, stages):
         @pl.loop(0, CHUNKS)
         def _(chunk):
             span = pl.multiple_of(chunk * 128, 128)
@@ -386,48 +391,52 @@
 
             one = reach1[:, pl.ds(span, 128)]
             two = reach2[:, pl.ds(span, 128)]
-            if 0 in levels and rate is None:
-                put_slots(0, both(0, [two] * 4, 1))
-            if 0 in levels:
-                x1 = one * inner(0, soft(0))
+            if 1 in stages:
+                if rate is None:
+                    put_slots(ROW0, both(0, [two] * 4, 1))
                 y1 = [two * s for s in soft(1)]
                 y2 = inner(1, y1)
+                put_sums(SUM1, both(1, y1, 1))
+                put_slots(ROW2, both(2, [y2] * 4, 1))
+                hold[1, :, pl.ds(span, 128)] = y2
+            if 2 in stages:
+                x1 = one * inner(0, soft(0))
                 put_slots(ROW1, both(1, [x1] * 4, -1))
-                put_sums(ROW1 + 32, both(1, y1, 1))
                 s2 = soft(2)
                 x2 = [x1 * s for s in s2]
+                put_sums(SUM2, both(2, x2, -1))
                 x3 = inner(2, x2)
-                put_slots(ROW2, both(2, [y2] * 4, 1))
-                put_sums(ROW2 + 32, both(2, x2, -1))
+                hold[0, :, pl.ds(span, 128)] = x3
                 for k in range(4):
                     strat[0, 8 * k : 8 * k + 8, pl.ds(span, 128)] = s2[k]
-            if 3 not in levels:
-                hold[0, :, pl.ds(span, 128)] = x3
-                hold[1, :, pl.ds(span, 128)] = y2
-                return
-            if 0 not in levels:
-                x3 = hold[0, :, pl.ds(span, 128)]
-                y2 = hold[1, :, pl.ds(span, 128)]
-            s3 = soft(3)
-            y3 = [y2 * s for s in s3]
-            put_slots(ROW3, both(3, [x3] * 4, -1))
-            put_sums(ROW3 + 32, both(3, y3, 1))
-            for k in range(4):
-                strat[1, 8 * k : 8 * k + 8, pl.ds(span, 128)] = s3[k]
-
-    def payoffs(top, end):
+            if 3 in stages:
+                if 2 not in stages:
+                    x3 = hold[0, :, pl.ds(span, 128)]
+                    y2 = hold[1, :, pl.ds(span, 128)]
+                s3 = soft(3)
+                y3 = [y2 * s for s in s3]
+                put_slots(ROW3, both(3, [x3] * 4, -1))
+                put_sums(SUM3, both(3, y3, 1))
+                for k in range(4):
+                    strat[1, 8 * k : 8 * k + 8, pl.ds(span, 128)] = s3[k]
+
+    def payoffs(top, end, up=None):
         sums = jnp.dot(folds[top:end, :], cards_tv[...], preferred_element_type=F32)
         for part, value in enumerate(three_parts(sums)):
             cols[top:end, PAD + 64 * part : PAD + 64 * part + 64] = value
+        total = jnp.zeros((8, 128), F32)
         for first in range(0, PAD, 256):
             last = min(first + 256, PAD)
             pay[top:end, first:last] = jnp.dot(
                 cols[top:end, :], blocks[:, first:last], preferred_element_type=F32
             )
+            if up is not None:
+                for span in range(first, last, 128):
+                    total = up(span, total)
+        return jnp.sum(total, axis=0, keepdims=True)
 
     def values_up(last):
-        def step(chunk, total):
-            span = pl.multiple_of(chunk * 128, 128)
+        def step(span, total):
             lively = 1.0 - dead_p[:, pl.ds(span, 128)]
 
             def pair(first_row):
@@ -451,9 +460,9 @@
                 return [values[k] + table[2, level, k] * below for k in range(4)]
 
             q3 = slots(ROW3)
-            q2 = joined(2, slots(ROW2), summed(ROW3 + 32))
-            q1 = joined(1, slots(ROW1), summed(ROW2 + 32) + weighted(1, q3))
-            q0 = joined(0, slots(0), summed(ROW1 + 32) + weighted(0, q2))
+            q2 = joined(2, slots(ROW2), summed(SUM3))
+            q1 = joined(1, slots(ROW1), summed(SUM2) + weighted(1, q3))
+            q0 = joined(0, slots(ROW0), summed(SUM1) + weighted(0, q2))
             for level, q in enumerate((q0, q1, q2, q3)):
                 if last:
                     for k in (0, 2):
@@ -467,8 +476,7 @@
                 total = total + ((q[0] * q[0] + q[1] * q[1]) + (q[2] * q[2] + q[3] * q[3]))
             return total
 
-        total = lax.fori_loop(0, CHUNKS, step, jnp.zeros((8, 128), F32))
-        return jnp.sum(total, axis=0, keepdims=True)
+        return step
 
     def exchange(src, ring, count, send_sem, recv_sem, peer):
         def copy(j):
@@ -496,8 +504,10 @@
         ring_a[0] = total
         return exchange(part_a, ring_a, PEERS_A, ar_send_a, recv_a, peer_a)
 
-    def reduce_second(finish, ring_a, ring_b, recv_b):
+    def reduce_second(finish, ring_a, ring_b, recv_b, ready=None):
         finish()
+        if ready is not None:
+            ready()
         total = jnp.sum(ring_a[...], axis=0)
         part_b[...] = total
         ring_b[0] = total
@@ -510,28 +520,28 @@
 
     sends[0].wait()
     gather(1, [(0, diffs.at[1]), (-1, win1)])
-    sends[1].wait()
-    sends[2].wait()
+    columns(None, (1,))
+    next_round(1)
+    payoffs(ROW0, ROW1)
+    heard(2, along_node, known_node)
+    announce(3, along_node, known_node)
+    for copy in sends[1:4]:
+        copy.wait()
     gather(0, [(0, diffs.at[0]), (-1, win0a), (-2, win0b)])
-    heard(1)
-    announce(2)
-    sends[3].wait()
     gather(2, [(0, diffs.at[2]), (1, win2)])
-    columns(None, (0, 1, 2))
-    heard(2)
-    announce(3)
-    payoffs(0, ROW3)
+    columns(None, (2,))
     sends[4].wait()
     sends[5].wait()
     gather(3, [(0, diffs.at[3]), (1, win3a), (2, win3b)])
     columns(None, (3,))
-    payoffs(ROW3, ROWS)
-    heard(3)
-    first = reduce_start(values_up(False), ring_a1, ar_recv_a1)
-    rate = reduce_rate(reduce_second(first, ring_a1, ring_b1, ar_recv_b1), ring_b1)
-    columns(rate, (0, 1, 2, 3))
-    payoffs(ROW1, ROWS)
-    first = reduce_start(values_up(True), ring_a2, ar_recv_a2)
+    total = payoffs(ROW1, ROWS, values_up(False))
+    heard(2, along_board, known_board)
+    first = reduce_start(total, ring_a1, ar_recv_a1)
+    ready = functools.partial(heard, 3, along_node, known_node)
+    rate = reduce_rate(reduce_second(first, ring_a1, ring_b1, ar_recv_b1, ready), ring_b1)
+    columns(rate, (1, 2, 3))
+    total = payoffs(SUM1, ROWS, values_up(True))
+    first = reduce_start(total, ring_a2, ar_recv_a2)
 
     def back(idx, src, dst, step):
         return pltpu.make_async_remote_copy(
@@ -582,6 +592,17 @@
     rate = reduce_rate(second, ring_b2)
     for level in range(LEVELS):
         out_logits[0, level] = own[level] + rate[0:1, 0:1] * out_values[0, level]
+
+
+def write_out(logits_v, values_v, out_logits, out_values, sem):
+    copies = [
+        pltpu.make_async_copy(logits_v, out_logits, sem.at[0]),
+        pltpu.make_async_copy(values_v, out_values, sem.at[1]),
+    ]
+    for copy in copies:
+        copy.start()
+    for copy in copies:
+        copy.wait()
 
 
 def per_device(
@@ -605,11 +626,11 @@
         vmem((PAD, 64), BF16),
         vmem((LEVELS, 24, PAD), F32),
         vmem((24, PAD), F32),
-        vmem((16, PAD), F32),
+        vmem((8, PAD), F32),
         vmem((16, PAD), F32),
         vmem((16, PAD), F32),
         vmem((24, PAD), F32),
-        vmem((8, PAD), F32),
+        vmem((16, PAD), F32),
         vmem((4,) + small, F32),
         vmem((4,) + small, jnp.int32),
         vmem((1, PAD), F32),
@@ -640,6 +661,7 @@
         vmem((16, PAD), F32),
         vmem((2, 8, PAD), F32),
         pltpu.SemaphoreType.REGULAR((4,)),
+        pltpu.SemaphoreType.REGULAR((3,)),
         dma((10,)),
         dma((14,)),
         dma((14,)),
@@ -657,7 +679,7 @@
     table = card_rows()
     turned = table.T.copy()
     turned[:, CARDS] = 1.0
-    return pl.pallas_call(
+    found = pl.pallas_call(
         kernel,
         name="extragradient",
         out_shape=(whole, whole),
@@ -684,6 +706,14 @@
             )
         ]
     )
+    return pl.pallas_call(
+        write_out,
+        name="write_out",
+        out_shape=(whole, whole),
+        in_specs=[free] * 2,
+        out_specs=(pl.BlockSpec(memory_space=pltpu.HBM),) * 2,
+        scratch_shapes=[dma((2,))],
+    )(*[pltpu.with_memory_space_constraint(value, pltpu.VMEM) for value in found])
 
 
 def solution(mesh):

time: 52.5 us -> 49.1 us (0.935)
  local copies, waits for them, and re-layouts: 1.72 us -> 0 us
  Pallas kernels: 50 us -> 48.3 us
    pallas_call x1, Pallas kernels: 50 us -> 47.2 us  [per_device(): pl.pallas_call(kernel, name='extragradient', out_shape=(whole, whole), in...]
    unnamed x2 -> x0, local copies, waits for them, and re-layouts: 1.72 us -> none
    pallas_call x0 -> x1, Pallas kernels: none -> 1.11 us  [per_device(): pl.pallas_call(write_out, name='write_out', out_shape=(whole, whole), in_...]
where the time goes in v3:
time: 49.1 us; the launch traced here: 49 us
  Pallas kernels  48.3 us (98%)
  between operations  0.64 us (1%)
    pallas_call x1, Pallas kernels, per_device(): pl.pallas_call(kernel, name='extragradient', out_shape=(whole, whole), in...  47.2 us
    pallas_call x1, Pallas kernels, per_device(): pl.pallas_call(write_out, name='write_out', out_shape=(whole, whole), in_...  1.11 us

profile of v3, /device:TPU:1, one launch (start us, length us, event | category | flops | bytes accessed | tf_op | source)
XLA Modules:
  0.0 49.0 jit_solution(15228570246044700557)
XLA Ops:
  0.6 47.2 %extragradient.1 = (f32[1,4,32,1326]{3,2,1,0:T(8,128)S(1)}, f32[1,4,32,1326]{3,2,1,0:T(8,128)S(1)}) custom-call(f32[1,4,32,1326]{3,2,1,0:T(8,128)} %logits.1, f32[4,32]{1,0:T(4,128)} %pot.1, s32[4,32]{1,0:T(4,128)} %kind.1, s32[4,32]{1,0:T(4,128)} %parent.1, f32[1,1326]{1,0:T(1,128)} %range_one.1, f32[1,1326]{1,0:T(1,128)} %range_two.1, s32[1,1326]{1,0:T(1,128)} %rank.1, ...), custom_call_target="tpu_custom_call" | custom-call | tf_op jit(solution)/shard_map/extragradient/pallas_call | solution.py:682
  47.9 1.1 %write_out.1 = (f32[1,4,32,1326]{3,2,1,0:T(8,128)}, f32[1,4,32,1326]{3,2,1,0:T(8,128)}) custom-call(f32[1,4,32,1326]{3,2,1,0:T(8,128)S(1)} %get-tuple-element.4.logits_v, f32[1,4,32,1326]{3,2,1,0:T(8,128)S(1)} %get-tuple-element.5.values_v), custom_call_target="tpu_custom_call" | custom-call | tf_op jit(solution)/shard_map/write_out/pallas_call | solution.py:709

commit v4 on v3

--- a/solution.py
+++ b/solution.py
@@ -273,9 +273,7 @@
         blocks[top : top + 48] = (-head * lively).astype(BF16)
         blocks[top + 48 : top + 64] = jnp.where(row == CARDS - 48, lively, -tail * lively).astype(BF16)
 
-    @pl.loop(0, CHUNKS)
-    def _(jb):
-        base = pl.multiple_of(jb * 128, 128)
+    for base in range(0, PAD, 128):
         rank_j = jnp.broadcast_to(rank_p[:, pl.ds(base, 128)], (128, 128)).T
         mine = cards_tv[pl.ds(base, 128)]
         for first in range(0, PAD, 256):
@@ -283,8 +281,9 @@
             shared = jnp.dot(mine, rhs_cards[:, first:last], preferred_element_type=F32)
             for start in range(first, last, 128):
                 span = slice(start, start + 128)
-                keep = shared[:, start - first : start - first + 128] < 0.5
-                order = jnp.clip(rank_p[:, span] - rank_j, -1.0, 1.0)
+                keep = shared[:, start - first : start - first + 128].astype(BF16) < 0.5
+                order = (rank_p[:, span] - rank_j).astype(BF16)
+                order = jnp.minimum(jnp.maximum(order, -1.0), 1.0)
                 blocks[pl.ds(base, 128), span] = jnp.where(keep, order, 0.0).astype(BF16)
 
     def offset(level):

time: 49.1 us -> 48.7 us (level)
  no operation moved by 1% of the time
where the time goes in v4:
time: 48.7 us; the launch traced here: 48.5 us
  Pallas kernels  47.9 us (98%)
  between operations  0.64 us (1%)
    pallas_call x1, Pallas kernels, per_device(): pl.pallas_call(kernel, name='extragradient', out_shape=(whole, whole), in...  46.8 us
    pallas_call x1, Pallas kernels, per_device(): pl.pallas_call(write_out, name='write_out', out_shape=(whole, whole), in_...  1.11 us

profile of v4, /device:TPU:1, one launch (start us, length us, event | category | flops | bytes accessed | tf_op | source)
XLA Modules:
  0.0 48.5 jit_solution(15960626624003054610)
XLA Ops:
  0.6 46.8 %extragradient.1 = (f32[1,4,32,1326]{3,2,1,0:T(8,128)S(1)}, f32[1,4,32,1326]{3,2,1,0:T(8,128)S(1)}) custom-call(f32[1,4,32,1326]{3,2,1,0:T(8,128)} %logits.1, f32[4,32]{1,0:T(4,128)} %pot.1, s32[4,32]{1,0:T(4,128)} %kind.1, s32[4,32]{1,0:T(4,128)} %parent.1, f32[1,1326]{1,0:T(1,128)} %range_one.1, f32[1,1326]{1,0:T(1,128)} %range_two.1, s32[1,1326]{1,0:T(1,128)} %rank.1, ...), custom_call_target="tpu_custom_call" | custom-call | tf_op jit(solution)/shard_map/extragradient/pallas_call | solution.py:681
  47.4 1.1 %write_out.1 = (f32[1,4,32,1326]{3,2,1,0:T(8,128)}, f32[1,4,32,1326]{3,2,1,0:T(8,128)}) custom-call(f32[1,4,32,1326]{3,2,1,0:T(8,128)S(1)} %get-tuple-element.4.logits_v, f32[1,4,32,1326]{3,2,1,0:T(8,128)S(1)} %get-tuple-element.5.values_v), custom_call_target="tpu_custom_call" | custom-call | tf_op jit(solution)/shard_map/write_out/pallas_call | solution.py:708
